TPU v7x, 32 devices: a whole 2x2x4 slice. The times are simulated.
32 devices in a mesh: cohort: 8 (over z, y), stripe: 4 (over x, core).
Axes of the slice: x: 2, y: 2, z: 4, core: 2. Of those that a mesh axis runs over, the one named last changes fastest.
Arguments:
- cohort_scores: bfloat16 [8, 18432, 256], P('cohort', 'stripe'), may hold values from -6 to 6
- allele_match: int32 [8, 18432], P('cohort', 'stripe'), may hold values from 0 to 18431, as said below
- allele_flip: int32 [8, 18432], P('cohort', 'stripe'), may hold values 0 or 1
- precision: float32 [8, 18432], P('cohort', 'stripe'), may hold values from 0.3 to 900
- reference_panel: bfloat16 [512, 18432], P(None, 'stripe'), may hold values from -20 to 20
- gene_weights: bfloat16 [64, 49, 4608], P('stripe'), may hold values from -0.09375 to 0.09375
- window_start: int32 [64], P('stripe'), may hold values from 0 to 17856, as said below
- window_length: int32 [64], P('stripe'), may hold values from 576 to 4608
Outputs:
- association: float32 [64, 49, 256], P('stripe', None, 'cohort')
Inputs may be any that keep to these rules, and one draw needn't show every extreme that they name: `allele_match`: within each cohort every variant is matched by exactly one row. The 4608 rows of one device match exactly 1152 variants of each stripe, stripe s being variants s * 4608 to (s + 1) * 4608 - 1. `window_start`: genes 16 * s to 16 * (s + 1) - 1 have their window start in stripe s; every window ends within the 18432 variants.
All inputs are finite; a program needn't handle non-finite values. No bound on the sum of `allele_flip` on one device may be relied on, other than what follows from the above.
Results may differ from a plain program's by a relative error of at most 0.004.
Values may be sent and summed in bfloat16 or wider, within the bound.
A program may use at most 128 MiB of HBM per device.

v0:
```python
import jax
import jax.numpy as jnp
from jax import lax
from jax.sharding import PartitionSpec as P

EPSILON = 1e-06


def passed_along(block, axis, distance):
    devices = range(lax.axis_size(axis))
    route = [(i - distance, i) for i in devices if i - distance in devices]
    return lax.ppermute(block, axis, route)


def on_device(
    cohort_scores,
    allele_match,
    allele_flip,
    precision,
    reference_panel,
    gene_weights,
    window_start,
    window_length,
):
    row_count = cohort_scores.shape[1]
    trait_count = cohort_scores.shape[2]
    stripe_count = lax.axis_size("stripe")
    cohort_count = lax.axis_size("cohort")
    bucket_rows = row_count // stripe_count
    block_traits = trait_count // cohort_count
    person_count = reference_panel.shape[0]
    gene_count = gene_weights.shape[0]
    tissue_count = gene_weights.shape[1]
    window_span = gene_weights.shape[2]
    step_width = min(512, window_span)
    first_variant = lax.axis_index("stripe") * row_count
    target = allele_match[0] // row_count
    inside = allele_match[0] - target * row_count
    member = (target[:, None] == jnp.arange(stripe_count, dtype=jnp.int32)[None, :]).astype(
        jnp.int32
    )
    ranking = jnp.sum(jnp.cumsum(member, axis=0) * member, axis=1) - 1
    placing = target * bucket_rows + ranking
    signs = (1 - 2 * allele_flip[0]).astype(jnp.bfloat16)
    flipped = cohort_scores[0] * signs[:, None]
    outgoing = jnp.zeros((row_count, trait_count), jnp.bfloat16).at[placing].set(flipped)
    out_keys = jnp.zeros((row_count,), jnp.int32).at[placing].set(inside)
    got_rows, got_keys = (
        lax.all_to_all(
            outgoing.reshape(stripe_count, bucket_rows, trait_count),
            "stripe",
            split_axis=0,
            concat_axis=0,
            tiled=True,
        ),
        lax.all_to_all(
            out_keys.reshape(stripe_count, bucket_rows),
            "stripe",
            split_axis=0,
            concat_axis=0,
            tiled=True,
        ),
    )
    aligned = (
        jnp.zeros((row_count, trait_count), jnp.bfloat16)
        .at[got_keys.reshape(row_count)]
        .set(got_rows.reshape(row_count, trait_count))
    )
    own_weight = precision[0]
    weighted = (jnp.sqrt(own_weight)[:, None] * aligned).astype(jnp.bfloat16)
    total_weight = lax.psum(own_weight, "cohort")
    received = lax.all_to_all(weighted, "cohort", split_axis=1, concat_axis=1, tiled=True)
    summed = jnp.sum(
        received.reshape(row_count, cohort_count, block_traits).astype(jnp.float32), axis=1
    )
    combined = (summed.T / jnp.sqrt(total_weight)[None, :]).astype(jnp.bfloat16)
    joined = jnp.concatenate([reference_panel, combined], axis=0)
    moved = passed_along(joined, "stripe", -1)
    panel_rim = moved[:person_count]
    score_rim = moved[person_count:]
    panel_ext = jnp.concatenate([reference_panel, panel_rim], axis=1)
    score_ext = jnp.concatenate([combined, score_rim], axis=1)

    def weight_block(gene, block, size):
        offset = block * step_width
        piece = lax.dynamic_slice(
            gene_weights[gene], (jnp.int32(0), offset), (tissue_count, step_width)
        )
        keep = offset + jnp.arange(step_width, dtype=jnp.int32) < size
        return jnp.where(keep[None, :], piece, jnp.zeros_like(piece))

    def window_variance(gene, size):
        begin = window_start[gene] - first_variant

        def add_block(block, running):
            columns = lax.dynamic_slice(
                panel_ext, (jnp.int32(0), begin + block * step_width), (person_count, step_width)
            )
            piece = weight_block(gene, block, size)
            return running + lax.dot_general(
                columns, piece, (((1,), (1,)), ((), ())), preferred_element_type=jnp.float32
            )

        blocks_needed = (size + step_width - 1) // step_width
        projected = lax.fori_loop(
            0, blocks_needed, add_block, jnp.zeros((person_count, tissue_count), jnp.float32)
        )
        return jnp.sum(projected * projected, axis=0) / person_count

    def window_score(gene):
        begin = window_start[gene] - first_variant
        size = window_length[gene]

        def add_block(block, running):
            window = lax.dynamic_slice(
                score_ext, (jnp.int32(0), begin + block * step_width), (block_traits, step_width)
            )
            piece = weight_block(gene, block, size)
            return running + lax.dot_general(
                piece, window, (((1,), (1,)), ((), ())), preferred_element_type=jnp.float32
            )

        blocks_needed = (size + step_width - 1) // step_width
        return lax.fori_loop(
            0, blocks_needed, add_block, jnp.zeros((tissue_count, block_traits), jnp.float32)
        )

    empty = jnp.zeros((gene_count, tissue_count), jnp.float32)

    def every_gene(gene, partial_value):
        return partial_value.at[gene].set(window_variance(gene, window_length[gene]))

    variance = lax.fori_loop(0, gene_count, every_gene, empty)

    def score_gene(gene, partial_value):
        return partial_value.at[gene].set(window_score(gene))

    numerator = lax.fori_loop(
        0, gene_count, score_gene, jnp.zeros((gene_count, tissue_count, block_traits), jnp.float32)
    )
    return numerator / jnp.sqrt(variance + EPSILON)[:, :, None]


def solution(mesh):
    in_specs = (
        P("cohort", "stripe", None),
        P("cohort", "stripe"),
        P("cohort", "stripe"),
        P("cohort", "stripe"),
        P(None, "stripe"),
        P("stripe", None, None),
        P("stripe"),
        P("stripe"),
    )
    out_specs = P("stripe", None, "cohort")
    return jax.shard_map(
        on_device, mesh=mesh, in_specs=in_specs, out_specs=out_specs, check_vma=False
    )
```

profile of v0, /device:TPU:1, one launch (start us, length us, event | category | flops | bytes accessed | tf_op | source)
XLA Modules:
  0.0 779.1 jit_solution(13550432650213802106)
XLA Ops:
  4.5 17.4 %scatter_custom_fusion = s32[4608]{0:T(1024)S(1)} fusion(s32[4608]{0:T(1024)S(1)} %fusion.23, s32[4608]{0:T(1024)S(1)} %get-tuple-element.875, s32[]{:T(128)} %constant.573.clone.1), kind=kCustom, calls=%fused_computation.65 | custom fusion | bytes 18436 | tf_op jit(solution)/shard_map/scatter | solution.py:47
  27.5 24.5 %scatter_custom_fusion.1 = bf16[4608,256]{1,0:T(8,128)(2,1)} fusion(s32[4608]{0:T(1024)S(1)} %fusion.23, bf16[1,4608,256]{2,1,0:T(8,128)(2,1)} %param.20, bf16[4608]{0:T(1024)(128)(2,1)S(1)} %convert_reduce_fusion.1, bf16[]{:T(256)} %constant.577.clone.1), kind=kCustom, calls=%fused_computation.32 | custom fusion | flops 1179648 | bytes 4728834 | tf_op jit(solution)/shard_map/scatter | solution.py:46
  55.9 27.3 %all-to-all-done.1 = bf16[4,1152,256]{2,1,0:T(8,128)(2,1)S(1)} async-done(((bf16[4,1152,256]{2,1,0:T(8,128)(2,1)}), bf16[4,1152,256]{2,1,0:T(8,128)(2,1)S(1)}, u32[]{:S(2)}, u32[]{:S(2)}) %all-to-all-start.1) | async-done | bytes 2359328 | tf_op jit(solution)/shard_map/all_to_all | solution.py:49
  84.6 21.1 %scatter_custom_fusion.2 = bf16[4608,256]{1,0:T(8,128)(2,1)S(1)} fusion(s32[4608]{0:T(1024)S(1)} %fusion.24, bf16[4608,256]{1,0:T(8,128)(2,1)} %bitcast.84, bf16[]{:T(256)} %constant.577.clone.1), kind=kCustom, calls=%fused_computation.34 | custom fusion | bytes 2359808 | tf_op jit(solution)/shard_map/scatter | solution.py:67
  119.2 69.8 %psum.7 = f32[4608]{0:T(1024)S(1)} all-reduce(f32[4608]{0:T(1024)S(1)} %reduce.34), channel_id=1, replica_groups=mesh['cohort'=8,'stripe'=4] {'cohort'}, use_global_device_ids=true, to_apply=%region_7.8 | all-reduce | flops 4608 | bytes 36864 | tf_op jit(solution)/shard_map/psum | solution.py:71
  194.3 10.3 %collective-permute-start = (bf16[544,4608]{1,0:T(8,128)(2,1)}, bf16[544,4608]{1,0:T(8,128)(2,1)}, u32[]{:S(2)}, u32[]{:S(2)}) collective-permute-start(bf16[544,4608]{1,0:T(8,128)(2,1)} %pad_maximum_fusion.1), channel_id=1, source_target_pairs={{1,0},{2,1},{3,2},{5,4},{6,5},{7,6},{9,8},{10,9},{11,10},{13,12},{... | collective-permute-start | bytes 15040520 | tf_op jit(solution)/shard_map/ppermute | solution.py:12
  204.6 10.2 %copy.16 = bf16[16,49,4608]{2,1,0:T(8,128)(2,1)} copy(bf16[16,49,4608]{2,0,1:T(8,128)(2,1)} %param.25) | data formatting | bytes 14450688 | tf_op jit(solution)/shard_map/while | solution.py:138
  214.8 45.2 %collective-permute-done = bf16[544,4608]{1,0:T(8,128)(2,1)} collective-permute-done((bf16[544,4608]{1,0:T(8,128)(2,1)}, bf16[544,4608]{1,0:T(8,128)(2,1)}, u32[]{:S(2)}, u32[]{:S(2)}) %collective-permute-start) | collective-permute-done | bytes 5013536 | tf_op jit(solution)/shard_map/ppermute | solution.py:12
  269.6 284.4 %while.117 = (s32[]{:T(128)}, f32[16,49]{1,0:T(8,128)S(1)}, s32[16]{0:T(128)S(1)}, s32[16]{0:T(128)S(1)}, s32[]{:T(128)}, /*index=5*/bf16[512,9216]{1,0:T(8,128)...) while((s32[]{:T(128)}, f32[16,49]{1,0:T(8,128)S(1)}, ...), condition=%wide.region_18.19_spmd, body=%wide.region_13.18_spmd.sunk | while | flops 25791580 | bytes 986578 | solution.py:133
  273.2 20.0 %while.119 = (s32[]{:T(128)}, f32[512,49]{0,1:T(8,128)S(1)}, s32[]{:T(128)}, s32[]{:T(128)}, bf16[512,9216]{1,0:T(8,128)(2,1)}, /*index=5*/s32[]{:T(128)}, bf16[...) while((s32[]{:T(128)}, f32[512,49]{0,1:T(8,128)S(1)}, ...), condition=%wide.region_16.16_spmd, body=%wide.region_15.15_spmd.sunk | while | flops 25741324 | bytes 784129 | solution.py:105
  308.7 8.9 %while.119 = (s32[]{:T(128)}, f32[512,49]{0,1:T(8,128)S(1)}, s32[]{:T(128)}, s32[]{:T(128)}, bf16[512,9216]{1,0:T(8,128)(2,1)}, /*index=5*/s32[]{:T(128)}, bf16[...) while((s32[]{:T(128)}, f32[512,49]{0,1:T(8,128)S(1)}, ...), condition=%wide.region_16.16_spmd, body=%wide.region_15.15_spmd.sunk | while | flops 25741324 | bytes 784129 | solution.py:105
  322.1 15.6 %while.119 = (s32[]{:T(128)}, f32[512,49]{0,1:T(8,128)S(1)}, s32[]{:T(128)}, s32[]{:T(128)}, bf16[512,9216]{1,0:T(8,128)(2,1)}, /*index=5*/s32[]{:T(128)}, bf16[...) while((s32[]{:T(128)}, f32[512,49]{0,1:T(8,128)S(1)}, ...), condition=%wide.region_16.16_spmd, body=%wide.region_15.15_spmd.sunk | while | flops 25741324 | bytes 784129 | solution.py:105
  342.1 15.6 %while.119 = (s32[]{:T(128)}, f32[512,49]{0,1:T(8,128)S(1)}, s32[]{:T(128)}, s32[]{:T(128)}, bf16[512,9216]{1,0:T(8,128)(2,1)}, /*index=5*/s32[]{:T(128)}, bf16[...) while((s32[]{:T(128)}, f32[512,49]{0,1:T(8,128)S(1)}, ...), condition=%wide.region_16.16_spmd, body=%wide.region_15.15_spmd.sunk | while | flops 25741324 | bytes 784129 | solution.py:105
  371.0 8.9 %while.119 = (s32[]{:T(128)}, f32[512,49]{0,1:T(8,128)S(1)}, s32[]{:T(128)}, s32[]{:T(128)}, bf16[512,9216]{1,0:T(8,128)(2,1)}, /*index=5*/s32[]{:T(128)}, bf16[...) while((s32[]{:T(128)}, f32[512,49]{0,1:T(8,128)S(1)}, ...), condition=%wide.region_16.16_spmd, body=%wide.region_15.15_spmd.sunk | while | flops 25741324 | bytes 784129 | solution.py:105
  384.3 8.9 %while.119 = (s32[]{:T(128)}, f32[512,49]{0,1:T(8,128)S(1)}, s32[]{:T(128)}, s32[]{:T(128)}, bf16[512,9216]{1,0:T(8,128)(2,1)}, /*index=5*/s32[]{:T(128)}, bf16[...) while((s32[]{:T(128)}, f32[512,49]{0,1:T(8,128)S(1)}, ...), condition=%wide.region_16.16_spmd, body=%wide.region_15.15_spmd.sunk | while | flops 25741324 | bytes 784129 | solution.py:105
  397.6 17.8 %while.119 = (s32[]{:T(128)}, f32[512,49]{0,1:T(8,128)S(1)}, s32[]{:T(128)}, s32[]{:T(128)}, bf16[512,9216]{1,0:T(8,128)(2,1)}, /*index=5*/s32[]{:T(128)}, bf16[...) while((s32[]{:T(128)}, f32[512,49]{0,1:T(8,128)S(1)}, ...), condition=%wide.region_16.16_spmd, body=%wide.region_15.15_spmd.sunk | while | flops 25741324 | bytes 784129 | solution.py:105
  419.8 15.6 %while.119 = (s32[]{:T(128)}, f32[512,49]{0,1:T(8,128)S(1)}, s32[]{:T(128)}, s32[]{:T(128)}, bf16[512,9216]{1,0:T(8,128)(2,1)}, /*index=5*/s32[]{:T(128)}, bf16[...) while((s32[]{:T(128)}, f32[512,49]{0,1:T(8,128)S(1)}, ...), condition=%wide.region_16.16_spmd, body=%wide.region_15.15_spmd.sunk | while | flops 25741324 | bytes 784129 | solution.py:105
  439.8 17.8 %while.119 = (s32[]{:T(128)}, f32[512,49]{0,1:T(8,128)S(1)}, s32[]{:T(128)}, s32[]{:T(128)}, bf16[512,9216]{1,0:T(8,128)(2,1)}, /*index=5*/s32[]{:T(128)}, bf16[...) while((s32[]{:T(128)}, f32[512,49]{0,1:T(8,128)S(1)}, ...), condition=%wide.region_16.16_spmd, body=%wide.region_15.15_spmd.sunk | while | flops 25741324 | bytes 784129 | solution.py:105
  462.1 20.0 %while.119 = (s32[]{:T(128)}, f32[512,49]{0,1:T(8,128)S(1)}, s32[]{:T(128)}, s32[]{:T(128)}, bf16[512,9216]{1,0:T(8,128)(2,1)}, /*index=5*/s32[]{:T(128)}, bf16[...) while((s32[]{:T(128)}, f32[512,49]{0,1:T(8,128)S(1)}, ...), condition=%wide.region_16.16_spmd, body=%wide.region_15.15_spmd.sunk | while | flops 25741324 | bytes 784129 | solution.py:105
  486.5 20.0 %while.119 = (s32[]{:T(128)}, f32[512,49]{0,1:T(8,128)S(1)}, s32[]{:T(128)}, s32[]{:T(128)}, bf16[512,9216]{1,0:T(8,128)(2,1)}, /*index=5*/s32[]{:T(128)}, bf16[...) while((s32[]{:T(128)}, f32[512,49]{0,1:T(8,128)S(1)}, ...), condition=%wide.region_16.16_spmd, body=%wide.region_15.15_spmd.sunk | while | flops 25741324 | bytes 784129 | solution.py:105
  511.0 11.1 %while.119 = (s32[]{:T(128)}, f32[512,49]{0,1:T(8,128)S(1)}, s32[]{:T(128)}, s32[]{:T(128)}, bf16[512,9216]{1,0:T(8,128)(2,1)}, /*index=5*/s32[]{:T(128)}, bf16[...) while((s32[]{:T(128)}, f32[512,49]{0,1:T(8,128)S(1)}, ...), condition=%wide.region_16.16_spmd, body=%wide.region_15.15_spmd.sunk | while | flops 25741324 | bytes 784129 | solution.py:105
  537.6 15.6 %while.119 = (s32[]{:T(128)}, f32[512,49]{0,1:T(8,128)S(1)}, s32[]{:T(128)}, s32[]{:T(128)}, bf16[512,9216]{1,0:T(8,128)(2,1)}, /*index=5*/s32[]{:T(128)}, bf16[...) while((s32[]{:T(128)}, f32[512,49]{0,1:T(8,128)S(1)}, ...), condition=%wide.region_16.16_spmd, body=%wide.region_15.15_spmd.sunk | while | flops 25741324 | bytes 784129 | solution.py:105
  554.1 224.3 %while.115 = (s32[]{:T(128)}, f32[16,49,32]{1,2,0:T(8,128)S(1)}, s32[16]{0:T(128)S(1)}, s32[16]{0:T(128)S(1)}, s32[]{:T(128)}, /*index=5*/bf16[16,49,4608]{2,1,0...) while((s32[]{:T(128)}, f32[16,49,32]{1,2,0:T(8,128)S(1)}, ...), condition=%wide.region_12.13_spmd, body=%wide.region_8.12_spmd.sunk | while | flops 1634928 | bytes 170554 | solution.py:138
  557.3 15.2 %while.118 = (s32[]{:T(128)}, f32[49,32]{0,1:T(8,128)S(1)}, s32[]{:T(128)}, s32[]{:T(128)}, bf16[16,49,4608]{2,1,0:T(8,128)(2,1)}, /*index=5*/s32[]{:T(128)}, s3...) while((s32[]{:T(128)}, f32[49,32]{0,1:T(8,128)S(1)}, ...), condition=%wide.region_11.11_spmd, body=%wide.region_10.10_spmd.sunk | while | flops 1633323 | bytes 114561 | solution.py:124
  595.9 11.9 %while.118 = (s32[]{:T(128)}, f32[49,32]{0,1:T(8,128)S(1)}, s32[]{:T(128)}, s32[]{:T(128)}, bf16[16,49,4608]{2,1,0:T(8,128)(2,1)}, /*index=5*/s32[]{:T(128)}, s3...) while((s32[]{:T(128)}, f32[49,32]{0,1:T(8,128)S(1)}, ...), condition=%wide.region_11.11_spmd, body=%wide.region_10.10_spmd.sunk | while | flops 1633323 | bytes 114561 | solution.py:124
  611.7 11.9 %while.118 = (s32[]{:T(128)}, f32[49,32]{0,1:T(8,128)S(1)}, s32[]{:T(128)}, s32[]{:T(128)}, bf16[16,49,4608]{2,1,0:T(8,128)(2,1)}, /*index=5*/s32[]{:T(128)}, s3...) while((s32[]{:T(128)}, f32[49,32]{0,1:T(8,128)S(1)}, ...), condition=%wide.region_11.11_spmd, body=%wide.region_10.10_spmd.sunk | while | flops 1633323 | bytes 114561 | solution.py:124
  655.9 13.6 %while.118 = (s32[]{:T(128)}, f32[49,32]{0,1:T(8,128)S(1)}, s32[]{:T(128)}, s32[]{:T(128)}, bf16[16,49,4608]{2,1,0:T(8,128)(2,1)}, /*index=5*/s32[]{:T(128)}, s3...) while((s32[]{:T(128)}, f32[49,32]{0,1:T(8,128)S(1)}, ...), condition=%wide.region_11.11_spmd, body=%wide.region_10.10_spmd.sunk | while | flops 1633323 | bytes 114561 | solution.py:124
  673.3 11.9 %while.118 = (s32[]{:T(128)}, f32[49,32]{0,1:T(8,128)S(1)}, s32[]{:T(128)}, s32[]{:T(128)}, bf16[16,49,4608]{2,1,0:T(8,128)(2,1)}, /*index=5*/s32[]{:T(128)}, s3...) while((s32[]{:T(128)}, f32[49,32]{0,1:T(8,128)S(1)}, ...), condition=%wide.region_11.11_spmd, body=%wide.region_10.10_spmd.sunk | while | flops 1633323 | bytes 114561 | solution.py:124
  689.1 13.6 %while.118 = (s32[]{:T(128)}, f32[49,32]{0,1:T(8,128)S(1)}, s32[]{:T(128)}, s32[]{:T(128)}, bf16[16,49,4608]{2,1,0:T(8,128)(2,1)}, /*index=5*/s32[]{:T(128)}, s3...) while((s32[]{:T(128)}, f32[49,32]{0,1:T(8,128)S(1)}, ...), condition=%wide.region_11.11_spmd, body=%wide.region_10.10_spmd.sunk | while | flops 1633323 | bytes 114561 | solution.py:124
  706.5 15.2 %while.118 = (s32[]{:T(128)}, f32[49,32]{0,1:T(8,128)S(1)}, s32[]{:T(128)}, s32[]{:T(128)}, bf16[16,49,4608]{2,1,0:T(8,128)(2,1)}, /*index=5*/s32[]{:T(128)}, s3...) while((s32[]{:T(128)}, f32[49,32]{0,1:T(8,128)S(1)}, ...), condition=%wide.region_11.11_spmd, body=%wide.region_10.10_spmd.sunk | while | flops 1633323 | bytes 114561 | solution.py:124
  725.5 15.2 %while.118 = (s32[]{:T(128)}, f32[49,32]{0,1:T(8,128)S(1)}, s32[]{:T(128)}, s32[]{:T(128)}, bf16[16,49,4608]{2,1,0:T(8,128)(2,1)}, /*index=5*/s32[]{:T(128)}, s3...) while((s32[]{:T(128)}, f32[49,32]{0,1:T(8,128)S(1)}, ...), condition=%wide.region_11.11_spmd, body=%wide.region_10.10_spmd.sunk | while | flops 1633323 | bytes 114561 | solution.py:124
  765.9 11.9 %while.118 = (s32[]{:T(128)}, f32[49,32]{0,1:T(8,128)S(1)}, s32[]{:T(128)}, s32[]{:T(128)}, bf16[16,49,4608]{2,1,0:T(8,128)(2,1)}, /*index=5*/s32[]{:T(128)}, s3...) while((s32[]{:T(128)}, f32[49,32]{0,1:T(8,128)S(1)}, ...), condition=%wide.region_11.11_spmd, body=%wide.region_10.10_spmd.sunk | while | flops 1633323 | bytes 114561 | solution.py:124
  (639 shorter events, 564.8 us)
Async XLA Ops:
  22.5 29.5 %all-to-all-start = ((s32[4,1,1152]{2,1,0:T(1,128)}), s32[4,1,1152]{2,1,0:T(1,128)S(1)}, u32[]{:S(2)}, u32[]{:S(2)}) async-start(s32[4,1,1152]{2,1,0:T(1,128)} %all_to_all.15), calls=%async_computation | async-start | bytes 36864 | tf_op jit(solution)/shard_map/all_to_all | solution.py:56
  52.0 3.8 copy-start.1
  52.0 31.2 %all-to-all-start.1 = ((bf16[4,1152,256]{2,1,0:T(8,128)(2,1)}), bf16[4,1152,256]{2,1,0:T(8,128)(2,1)S(1)}, u32[]{:S(2)}, u32[]{:S(2)}) async-start(bf16[4,1152,256]{2,1,0:T(8,128)(2,1)} %bitcast.15), calls=%async_computation.1 | async-start | bytes 4718592 | tf_op jit(solution)/shard_map/all_to_all | solution.py:49
  83.2 1.4 copy-start
  113.1 75.9 %all-to-all-start.2 = ((bf16[4608,8,32]{0,2,1:T(8,128)(2,1)}), bf16[4608,8,32]{0,2,1:T(8,128)(2,1)S(1)}, u32[]{:S(2)}, u32[]{:S(2)}) async-start(bf16[4608,8,32]{0,2,1:T(8,128)(2,1)} %bitcast.83), calls=%async_computation.2 | async-start | bytes 4718592 | tf_op jit(solution)/shard_map/all_to_all | solution.py:72
  194.3 65.8 %collective-permute-start = (bf16[544,4608]{1,0:T(8,128)(2,1)}, bf16[544,4608]{1,0:T(8,128)(2,1)}, u32[]{:S(2)}, u32[]{:S(2)}) collective-permute-start(bf16[544,4608]{1,0:T(8,128)(2,1)} %pad_maximum_fusion.1), channel_id=1, source_target_pairs={{1,0},{2,1},{3,2},{5,4},{6,5},{7,6},{9,8},{10,9},{11,10},{13,12},{... | collective-permute-start | bytes 15040520 | tf_op jit(solution)/shard_map/ppermute | solution.py:12
  261.0 3.6 slice-start
  261.1 3.7 slice-start.1
  264.8 4.8 copy-start.3
  264.8 4.8 copy-start.4
  264.8 4.8 copy-start.5
  269.6 284.5 %copy-start.2 = (s32[3]{0:T(128)S(1)}, s32[3]{0:T(128)}, u32[]{:S(2)}) copy-start(s32[3]{0:T(128)} %constant.545.clone.1) | copy-start | bytes 40
where the time goes:
time: 786 us; the launch traced here: 779 us
  matrix products  249 us (32%)
  other arithmetic  214 us (27%)
  local copies, waits for them, and re-layouts  101 us (13%)
  waiting for transfers between devices  72.6 us (9%)
  blocking collectives  69.8 us (9%)
  loops' own time  48.4 us (6%)
  starting transfers between devices  24.4 us (3%)
    dot_general x96, matrix products, add_block(): lax.dot_general(columns, piece, (((1,), (1,)), ((), ())), preferred_eleme...  143 us
    lt x192, other arithmetic, weight_block(): keep = offset + jnp.arange(step_width, dtype=jnp.int32) < size  122 us
    dot_general x96, matrix products, add_block(): lax.dot_general(piece, window, (((1,), (1,)), ((), ())), preferred_elemen...  106 us
    psum x1, blocking collectives, on_device(): total_weight = lax.psum(own_weight, 'cohort')  69.8 us
    ppermute x1, waiting for transfers between devices, passed_along(): return lax.ppermute(block, axis, route)  45.2 us
    another operation x50, other arithmetic  37.1 us
    all_to_all x1, waiting for transfers between devices, on_device(): lax.all_to_all(outgoing.reshape(stripe_count, bucket_rows, trait_count),...  27.3 us
    scatter x1, other arithmetic, on_device(): jnp.zeros((row_count, trait_count), jnp.bfloat16).at[placing].set(flipped)  24.5 us
  transfers between devices with their start and end apart: 4, of which 2 were waited for; matrix products, arithmetic and copies ran while one was open for 5% of the time, Pallas kernels for 0%

commit v1 on v0

--- a/solution.py
+++ b/solution.py
@@ -1,6 +1,10 @@
+import functools
+
 import jax
 import jax.numpy as jnp
 from jax import lax
+from jax.experimental import pallas as pl
+from jax.experimental.pallas import tpu as pltpu
 from jax.sharding import PartitionSpec as P
 
 EPSILON = 1e-06
@@ -12,7 +16,7 @@
     return lax.ppermute(block, axis, route)
 
 
-def on_device(
+def general_device(
     cohort_scores,
     allele_match,
     allele_flip,
@@ -141,6 +145,417 @@
     return numerator / jnp.sqrt(variance + EPSILON)[:, :, None]
 
 
+MESH = pl.DeviceIdType.MESH
+BF16 = jnp.bfloat16
+F32 = jnp.float32
+Y_COUNT = 2
+CHUNKS = 6
+
+
+def pack_kernel(low_ref, high_ref, left_ref, slot_ref, out_ref, total):
+    block = pl.program_id(0)
+    width = out_ref.shape[2]
+    depth = left_ref.shape[1] // 4
+    total[...] = jnp.zeros_like(total)
+    lane = lax.broadcasted_iota(jnp.int32, (depth, 128), 1) + block * width
+
+    def add_rows(k, carry):
+        start = pl.multiple_of(k * depth, depth)
+        slots = slot_ref[pl.ds(start, depth), :]
+        chosen = jnp.concatenate(
+            [
+                jnp.where(slots == lane + 128 * b, 1.0, 0.0).astype(BF16)
+                for b in range(width // 128)
+            ],
+            axis=1,
+        )
+        total[...] += jnp.dot(
+            left_ref[:, pl.ds(start, depth)], chosen, preferred_element_type=F32
+        )
+        return carry
+
+    lax.fori_loop(low_ref[block], high_ref[block], add_rows, 0)
+    out_ref[0] = total[...].astype(BF16)
+
+
+def pack_rows(left, slot, low, high, stripes):
+    height, rows = left.shape
+    bucket = rows // stripes
+    width = bucket // 3
+    return pl.pallas_call(
+        pack_kernel,
+        grid_spec=pltpu.PrefetchScalarGridSpec(
+            num_scalar_prefetch=2,
+            grid=(stripes * 3,),
+            in_specs=[
+                pl.BlockSpec((height, rows), lambda i, lo, hi: (0, 0)),
+                pl.BlockSpec((rows, 128), lambda i, lo, hi: (0, 0)),
+            ],
+            out_specs=pl.BlockSpec((1, height, width), lambda i, lo, hi: (i // 3, 0, i % 3)),
+            scratch_shapes=[pltpu.VMEM((height, width), F32)],
+        ),
+        out_shape=jax.ShapeDtypeStruct((stripes, height, bucket), BF16),
+        cost_estimate=pl.CostEstimate(
+            flops=height * rows * rows, bytes_accessed=4 * height * rows, transcendentals=0
+        ),
+    )(low, high, left, slot)
+
+
+def combine_kernel(
+    z_count,
+    got_ref,
+    key_ref,
+    precision_ref,
+    out_ref,
+    own,
+    y_got,
+    pair,
+    z_got,
+    weights,
+    root,
+    total,
+    y_send,
+    y_recv,
+    z_send,
+    z_recv,
+    w_send,
+    w_recv,
+):
+    cohort = lax.axis_index("cohort")
+    stripe = lax.axis_index("stripe")
+    cohorts = z_count * Y_COUNT
+    z, y = cohort // Y_COUNT, lax.rem(cohort, Y_COUNT)
+    stripes, traits, bucket = got_ref.shape
+    block = traits // cohorts
+    width = own.shape[4]
+
+    barrier = pltpu.get_barrier_semaphore()
+    for d in range(1, cohorts):
+        pl.semaphore_signal(
+            barrier, inc=1, device_id=(lax.rem(cohort + d, cohorts), stripe), device_id_type=MESH
+        )
+    pl.semaphore_wait(barrier, cohorts - 1)
+
+    def weight_copy(d):
+        return pltpu.make_async_remote_copy(
+            src_ref=precision_ref,
+            dst_ref=weights.at[d],
+            send_sem=w_send.at[d],
+            recv_sem=w_recv.at[d],
+            device_id=(lax.rem(cohort + d, cohorts), stripe),
+            device_id_type=MESH,
+        )
+
+    def y_copy(k):
+        return pltpu.make_async_remote_copy(
+            src_ref=own.at[k, 1 - y],
+            dst_ref=y_got.at[k],
+            send_sem=y_send.at[k],
+            recv_sem=y_recv.at[k],
+            device_id=(z * Y_COUNT + 1 - y, stripe),
+            device_id_type=MESH,
+        )
+
+    def z_copy(k, d):
+        other = lax.rem(z + d, z_count)
+        return pltpu.make_async_remote_copy(
+            src_ref=pair.at[k, other],
+            dst_ref=z_got.at[k, d],
+            send_sem=z_send.at[k, d],
+            recv_sem=z_recv.at[k, d],
+            device_id=(other * Y_COUNT + y, stripe),
+            device_id_type=MESH,
+        )
+
+    for d in range(1, cohorts):
+        weight_copy(d).start()
+    root[...] = jnp.sqrt(precision_ref[...])
+
+    def step(k, carry):
+        @pl.when(k < CHUNKS)
+        def _():
+            lane = lax.broadcasted_iota(jnp.int32, (bucket, 128), 1) + k * width
+            total[...] = jnp.zeros_like(total)
+
+            def add_source(s, inner):
+                keys = key_ref[pl.ds(pl.multiple_of(s * bucket, bucket), bucket), :]
+                chosen = jnp.concatenate(
+                    [
+                        jnp.where(keys == lane + 128 * b, 1.0, 0.0).astype(BF16)
+                        for b in range(width // 128)
+                    ],
+                    axis=1,
+                )
+                total[...] += jnp.dot(got_ref[s], chosen, preferred_element_type=F32)
+                return inner
+
+            lax.fori_loop(0, stripes, add_source, 0)
+            scale = root[:, pl.ds(pl.multiple_of(k * width, width), width)]
+            for c in range(cohorts):
+                own[k, c % Y_COUNT, c // Y_COUNT] = (
+                    total[c * block : (c + 1) * block, :] * scale
+                ).astype(BF16)
+            y_copy(k).start()
+
+        @pl.when(k >= 1)
+        def _():
+            last = k - 1
+            y_copy(last).wait_recv()
+            for zi in range(z_count):
+                pair[last, zi] = (
+                    own[last, y, zi].astype(F32) + y_got[last, zi].astype(F32)
+                ).astype(BF16)
+            for d in range(1, z_count):
+                z_copy(last, d).start()
+
+        return carry
+
+    lax.fori_loop(0, CHUNKS + 1, step, 0)
+
+    weight_sum = precision_ref[...]
+    for d in range(1, cohorts):
+        weight_copy(d).wait_recv()
+        weight_sum = weight_sum + weights[d]
+    root[...] = jnp.sqrt(weight_sum)
+
+    def finish(k, carry):
+        summed = pair[k, z].astype(F32)
+        for d in range(1, z_count):
+            z_copy(k, d).wait_recv()
+            summed = summed + z_got[k, d].astype(F32)
+        here = pl.ds(pl.multiple_of(k * width, width), width)
+        out_ref[:, here] = (summed / root[:, here]).astype(BF16)
+        y_copy(k).wait_send()
+        for d in range(1, z_count):
+            z_copy(k, d).wait_send()
+        return carry
+
+    lax.fori_loop(0, CHUNKS, finish, 0)
+    for d in range(1, cohorts):
+        weight_copy(d).wait_send()
+
+
+def combine(got, keys, precision, cohorts):
+    stripes, traits, bucket = got.shape
+    rows = stripes * bucket
+    width = rows // CHUNKS
+    block = traits // cohorts
+    z_count = cohorts // Y_COUNT
+    vmem = pl.BlockSpec(memory_space=pltpu.VMEM)
+    dma = pltpu.SemaphoreType.DMA
+    return pl.pallas_call(
+        functools.partial(combine_kernel, z_count),
+        out_shape=jax.ShapeDtypeStruct((block, rows), BF16),
+        in_specs=[vmem] * 3,
+        out_specs=vmem,
+        scratch_shapes=[
+            pltpu.VMEM((CHUNKS, Y_COUNT, z_count, block, width), BF16),
+            pltpu.VMEM((CHUNKS, z_count, block, width), BF16),
+            pltpu.VMEM((CHUNKS, z_count, block, width), BF16),
+            pltpu.VMEM((CHUNKS, z_count, block, width), BF16),
+            pltpu.VMEM((cohorts, 1, rows), F32),
+            pltpu.VMEM((1, rows), F32),
+            pltpu.VMEM((traits, width), F32),
+            dma((CHUNKS,)),
+            dma((CHUNKS,)),
+            dma((CHUNKS, z_count)),
+            dma((CHUNKS, z_count)),
+            dma((cohorts,)),
+            dma((cohorts,)),
+        ],
+        compiler_params=pltpu.CompilerParams(collective_id=0, has_side_effects=True),
+    )(got, keys, precision)
+
+
+def window_product(begin, size, weight_ref, side_ref, total):
+    span = weight_ref.shape[2]
+    step = span // 4
+    blocks = step // 128
+    shift = lax.rem(begin, 128)
+    base = begin - shift
+    lane = lax.broadcasted_iota(jnp.int32, (weight_ref.shape[1], 128), 1)
+    total[...] = jnp.zeros_like(total)
+
+    def add_part(part, carry):
+        first = part * blocks
+
+        def turned(b):
+            at = jnp.clip(first + b, 0, span // 128 - 1)
+            piece = weight_ref[0, :, pl.ds(pl.multiple_of(at * 128, 128), 128)]
+            return pltpu.roll(piece.astype(F32), shift, 1)
+
+        before = turned(-1)
+        made = []
+        for b in range(blocks):
+            after = turned(b)
+            place = (first + b) * 128 + lane - shift
+            keep = jnp.logical_and(place >= 0, place < size)
+            made.append(
+                jnp.where(keep, jnp.where(lane < shift, before, after), 0.0).astype(BF16)
+            )
+            before = after
+        columns = side_ref[:, pl.ds(pl.multiple_of(base + first * 128, 128), step)]
+        total[...] += lax.dot_general(
+            jnp.concatenate(made, axis=1),
+            columns,
+            (((1,), (1,)), ((), ())),
+            preferred_element_type=F32,
+        )
+        return carry
+
+    lax.fori_loop(0, (size + shift + step - 1) // step, add_part, 0)
+
+
+def variance_kernel(begin_ref, size_ref, weight_ref, side_ref, out_ref, total):
+    gene = pl.program_id(0)
+    window_product(begin_ref[gene], size_ref[gene], weight_ref, side_ref, total)
+    projected = total[...]
+    out_ref[0] = jnp.sum(projected * projected, axis=1, keepdims=True)
+
+
+def score_kernel(begin_ref, size_ref, weight_ref, side_ref, variance_ref, out_ref, total):
+    gene = pl.program_id(0)
+    window_product(begin_ref[gene], size_ref[gene], weight_ref, side_ref, total)
+    out_ref[0] = total[...] / jnp.sqrt(variance_ref[0] + EPSILON)
+
+
+def by_gene(kernel, begin, size, weights, side, extra, width):
+    genes, tissues, span = weights.shape
+    column = pl.BlockSpec((1, tissues, 1), lambda g, b, s: (g, 0, 0))
+    return pl.pallas_call(
+        kernel,
+        grid_spec=pltpu.PrefetchScalarGridSpec(
+            num_scalar_prefetch=2,
+            grid=(genes,),
+            in_specs=[
+                pl.BlockSpec((1, tissues, span), lambda g, b, s: (g, 0, 0)),
+                pl.BlockSpec(side.shape, lambda g, b, s: (0, 0)),
+            ]
+            + [column] * len(extra),
+            out_specs=pl.BlockSpec((1, tissues, width), lambda g, b, s: (g, 0, 0)),
+            scratch_shapes=[pltpu.VMEM((tissues, side.shape[0]), F32)],
+        ),
+        out_shape=jax.ShapeDtypeStruct((genes, tissues, width), F32),
+        cost_estimate=pl.CostEstimate(
+            flops=2 * genes * tissues * span * side.shape[0],
+            bytes_accessed=2 * genes * tissues * span,
+            transcendentals=0,
+        ),
+    )(begin, size, weights, side, *extra)
+
+
+def extended(block, step):
+    rim = passed_along(block, "stripe", -1)
+    return jnp.concatenate([block, rim, jnp.zeros((block.shape[0], step), BF16)], axis=1)
+
+
+def fast_device(
+    cohort_scores,
+    allele_match,
+    allele_flip,
+    precision,
+    reference_panel,
+    gene_weights,
+    window_start,
+    window_length,
+):
+    row_count, trait_count = cohort_scores.shape[1:]
+    stripes = lax.axis_size("stripe")
+    cohorts = lax.axis_size("cohort")
+    bucket = row_count // stripes
+    persons = reference_panel.shape[0]
+    step = gene_weights.shape[2] // 4
+    begin = window_start - lax.axis_index("stripe") * row_count
+
+    share = persons // cohorts
+    panel = lax.dynamic_slice_in_dim(
+        reference_panel, lax.axis_index("cohort") * share, share, axis=0
+    )
+    panel_ext = extended(panel, step)
+
+    match = allele_match[0]
+    target = match // row_count
+    inside = match - target * row_count
+    member = target[None, :] == jnp.arange(stripes, dtype=jnp.int32)[:, None]
+    ranking = jnp.cumsum(member.astype(jnp.int32), axis=1)
+    rank = jnp.sum(jnp.where(member, ranking, 0), axis=0) - 1
+    slot = target * bucket + rank
+    width = bucket // 3
+    depth = row_count // 4
+    ends = ranking[:, depth - 1 :: depth]
+    edges = jnp.arange(3, dtype=jnp.int32) * width
+    low = jnp.sum(ends[:, None, :] <= edges[None, :, None], axis=2, dtype=jnp.int32)
+    high = 1 + jnp.sum(ends[:, None, :] < (edges + width)[None, :, None], axis=2, dtype=jnp.int32)
+    signs = (1 - 2 * allele_flip[0]).astype(BF16)
+    left = jnp.concatenate(
+        [
+            (cohort_scores[0] * signs[:, None]).T,
+            (inside // 64).astype(BF16)[None, :],
+            lax.rem(inside, 64).astype(BF16)[None, :],
+            jnp.zeros((14, row_count), BF16),
+        ],
+        axis=0,
+    )
+    outgoing = pack_rows(
+        left,
+        jnp.broadcast_to(slot[:, None], (row_count, 128)),
+        low.reshape(-1),
+        high.reshape(-1),
+        stripes,
+    )
+    got = lax.all_to_all(outgoing, "stripe", split_axis=0, concat_axis=0, tiled=True)
+
+    squares = by_gene(variance_kernel, begin, window_length, gene_weights, panel_ext, (), 1)
+    shares = lax.all_to_all(
+        jnp.broadcast_to(squares[:, :, 0][None], (cohorts,) + squares.shape[:2]),
+        "cohort",
+        split_axis=0,
+        concat_axis=0,
+        tiled=True,
+    )
+    variance = jnp.sum(shares, axis=0)[:, :, None] / persons
+
+    keys = (
+        64 * got[:, trait_count].astype(jnp.int32) + got[:, trait_count + 1].astype(jnp.int32)
+    ).reshape(row_count)
+    combined = combine(
+        got[:, :trait_count],
+        jnp.broadcast_to(keys[:, None], (row_count, 128)),
+        precision,
+        cohorts,
+    )
+    score_ext = extended(combined, step)
+    return by_gene(
+        score_kernel,
+        begin,
+        window_length,
+        gene_weights,
+        score_ext,
+        (variance,),
+        combined.shape[0],
+    )
+
+
+def on_device(cohort_scores, *others):
+    rows, traits = cohort_scores.shape[1:]
+    stripes = lax.axis_size("stripe")
+    cohorts = lax.axis_size("cohort")
+    span = others[4].shape[2]
+    fits = (
+        cohorts % Y_COUNT == 0
+        and traits % (16 * cohorts) == 0
+        and rows % (384 * stripes) == 0
+        and rows % (128 * CHUNKS) == 0
+        and rows < 16384
+        and span % 512 == 0
+        and span <= rows
+        and others[3].shape[0] % (16 * cohorts) == 0
+    )
+    if fits:
+        return fast_device(cohort_scores, *others)
+    return general_device(cohort_scores, *others)
+
+
 def solution(mesh):
     in_specs = (
         P("cohort", "stripe", None),

time: 786 us -> 177 us (0.23)
  matrix products: 249 us -> 0 us
  other arithmetic: 214 us -> 12.6 us
  Pallas kernels: 0 us -> 95.9 us
  local copies, waits for them, and re-layouts: 101 us -> 27.6 us
  blocking collectives: 69.8 us -> 10.1 us
  waiting for transfers between devices: 72.6 us -> 17.1 us
  loops' own time: 48.4 us -> 0 us
  starting transfers between devices: 24.4 us -> 12 us
    dot_general x192 -> x0, matrix products: 249 us -> none  [the longest x96 143 us: add_block(): lax.dot_general(columns, piece, (((1,), (1,)), ((), ())), preferred_eleme...]
    lt x192 -> x0, other arithmetic: 122 us -> none  [weight_block(): keep = offset + jnp.arange(step_width, dtype=jnp.int32) < size]
    pallas_call x0 -> x4, Pallas kernels: none -> 95.9 us  [the longest x1 40.3 us: combine(): pl.pallas_call(functools.partial(combine_kernel, z_count), out_shape=jax....]
    psum x1 -> x0, blocking collectives: 69.8 us -> none  [on_device(): total_weight = lax.psum(own_weight, 'cohort')]
    another operation x34 -> x0, loops' own time: 48.4 us -> none  [the longest x1 23.2 us: on_device(): variance = lax.fori_loop(0, gene_count, every_gene, empty)]
    ppermute x1 -> x2, waiting for transfers between devices: 45.2 us -> 0.01 us  [passed_along(): return lax.ppermute(block, axis, route)]
    dynamic_slice x64 -> x1, local copies, waits for them, and re-layouts: 40.5 us -> 1.1 us  [fast_device(): lax.dynamic_slice_in_dim(reference_panel, lax.axis_index('cohort') * shar...]
    scatter x18 -> x0, local copies, waits for them, and re-layouts: 39.1 us -> none  [the longest x1 21.1 us: on_device(): aligned = jnp.zeros((row_count, trait_count), jnp.bfloat16).at[got_keys.r...]
  transfers between devices with their start and end apart: 4 -> 3, of which waited for: 2 -> 1; matrix products, arithmetic and copies ran while one was open for 5% -> 18% of each run, Pallas kernels for 0% -> 21%
where the time goes in v1:
time: 177 us; the launch traced here: 175 us
  Pallas kernels  95.9 us (54%)
  local copies, waits for them, and re-layouts  27.6 us (16%)
  waiting for transfers between devices  17.1 us (10%)
  other arithmetic  12.6 us (7%)
  starting transfers between devices  12 us (7%)
  blocking collectives  10.1 us (6%)
    pallas_call x1, Pallas kernels, combine(): pl.pallas_call(functools.partial(combine_kernel, z_count), out_shape=jax....  40.3 us
    pallas_call x2, Pallas kernels, by_gene(): pl.pallas_call(kernel, grid_spec=pltpu.PrefetchScalarGridSpec(num_scalar_...  37.9 us
    pallas_call x1, Pallas kernels, pack_rows(): pl.pallas_call(pack_kernel, grid_spec=pltpu.PrefetchScalarGridSpec(num_sc...  17.7 us
    all_to_all x1, waiting for transfers between devices, fast_device(): lax.all_to_all(outgoing, 'stripe', split_axis=0, concat_axis=0, tiled=True)  17.1 us
    unnamed x11, local copies, waits for them, and re-layouts  13.3 us
    all_to_all x1, blocking collectives, fast_device(): lax.all_to_all(jnp.broadcast_to(squares[:, :, 0][None], (cohorts,) + squa...  10.1 us
    ppermute x2, starting transfers between devices, passed_along(): return lax.ppermute(block, axis, route)  6.81 us
    all_to_all x1, starting transfers between devices, fast_device(): lax.all_to_all(outgoing, 'stripe', split_axis=0, concat_axis=0, tiled=True)  5.15 us
  transfers between devices with their start and end apart: 3, of which 1 were waited for; matrix products, arithmetic and copies ran while one was open for 18% of the time, Pallas kernels for 21%

profile of v1, /device:TPU:1, one launch (start us, length us, event | category | flops | bytes accessed | tf_op | source)
XLA Modules:
  0.0 175.4 jit_solution(194580595100798836)
XLA Ops:
  0.0 1.1 constant_dynamic-slice_fusion
  1.1 1.9 %collective-permute-start.1 = (bf16[64,4608]{1,0:T(8,128)(2,1)S(1)}, bf16[64,4608]{1,0:T(8,128)(2,1)}, u32[]{:S(2)}, u32[]{:S(2)}) collective-permute-start(bf16[64,4608]{1,0:T(8,128)(2,1)S(1)} %constant_dynamic-slice_fusion), channel_id=1, source_target_pairs={{1,0},{2,1},{3,2},{5,4},{6,5},{7,6},{9,8},{10,9},{11,10},{13,12},{... | collective-permute-start | bytes 1769480 | tf_op jit(solution)/shard_map/ppermute | solution.py:16
  3.0 0.9 fusion.7
  4.0 0.9 fusion.9
  4.8 0.9 fusion.10
  5.8 1.2 reduce-window.6
  6.9 0.2 slice_reduce_fusion
  7.6 0.2 convert_reduce_fusion.1
  8.0 0.7 add.52.high_ref
  8.7 0.6 reshape.120.low_ref
  9.4 2.8 %copy.20 = bf16[1,4608,256]{1,2,0:T(8,128)(2,1)S(1)} copy(bf16[1,4608,256]{2,1,0:T(8,128)(2,1)} %param.8) | data formatting | bytes 4718592 | tf_op args[0]
  12.5 2.0 %maximum_maximum_fusion.left_ref = bf16[272,4608]{1,0:T(8,128)(2,1)} fusion(bf16[1,4608]{1,0:T(2,128)(2,1)S(1)} %convert_element_type.50, bf16[1,4608]{1,0:T(2,128)(2,1)S(1)} %get-tuple-element.9, bf16[256,4608]{1,0:T(8,128)(2,1)S(1)} %fusion, bf16[272]{0:T(512)(128)(2,1)S(1)} %pad.9.clone), kind=kLoop, calls=%fused_computation | loop fusion | flops 10027008 | bytes 4885024 | tf_op jit(solution)/shard_map/concatenate | solution.py:490
  14.6 3.1 %broadcast_in_dim.20.slot_ref = s32[4608,128]{1,0:T(8,128)} broadcast(s32[4608]{0:T(1024)S(1)} %fusion.3), dimensions={0} | broadcast | bytes 2377728 | tf_op jit(solution)/shard_map/broadcast_in_dim | solution.py:501
  17.7 17.7 %shard_map.82 = bf16[4,272,1152]{2,1,0:T(8,128)(2,1)} custom-call(s32[12]{0:T(128)} %reshape.120.low_ref, s32[12]{0:T(128)} %add.52.high_ref, bf16[272,4608]{1,0:T(8,128)(2,1)} %maximum_maximum_fusion.left_ref, s32[4608,128]{1,0:T(8,128)} %broadcast_in_dim.20.slot_ref), custom_call_target="tpu_custom_call" | custom-call | flops 5775556608 | bytes 5013504 | tf_op jit(solution)/shard_map/pallas_call | solution.py:185
  35.3 5.2 %all-to-all-start = ((bf16[4,272,1152]{2,1,0:T(8,128)(2,1)}), bf16[4,272,1152]{2,1,0:T(8,128)(2,1)S(1)}, u32[]{:S(2)}, u32[]{:S(2)}) async-start(bf16[4,272,1152]{2,1,0:T(8,128)(2,1)} %shard_map.82), calls=%async_computation | async-start | bytes 5013504 | tf_op jit(solution)/shard_map/all_to_all | solution.py:506
  40.5 10.2 %copy.22.weight_ref = bf16[16,49,4608]{2,1,0:T(8,128)(2,1)} copy(bf16[16,49,4608]{2,0,1:T(8,128)(2,1)} %param.13) | data formatting | bytes 14450688 | tf_op args[5]
  50.7 0.5 broadcast_subtract_fusion.begin_ref
  51.2 2.4 %maximum_maximum_fusion.1.side_ref = bf16[64,10368]{1,0:T(8,128)(2,1)} fusion(bf16[64,4608]{1,0:T(8,128)(2,1)} %collective-permute-done.1, bf16[64,4608]{1,0:T(8,128)(2,1)S(1)} %constant_dynamic-slice_fusion, bf16[10368]{0:T(1024)(128)(2,1)S(1)} %pad.5.clone), kind=kLoop, calls=%fused_computation.3 | loop fusion | flops 3981312 | bytes 2527488 | tf_op jit(solution)/shard_map/concatenate | solution.py:449
  53.6 17.1 %all-to-all-done = bf16[4,272,1152]{2,1,0:T(8,128)(2,1)S(1)} async-done(((bf16[4,272,1152]{2,1,0:T(8,128)(2,1)}), bf16[4,272,1152]{2,1,0:T(8,128)(2,1)S(1)}, u32[]{:S(2)}, u32[]{:S(2)}) %all-to-all-start) | async-done | bytes 2506784 | tf_op jit(solution)/shard_map/all_to_all | solution.py:506
  70.8 1.6 slice.25.got_ref
  72.5 3.1 %broadcast_in_dim.21.key_ref = s32[4608,128]{1,0:T(8,128)} broadcast(s32[4608]{0:T(1024)S(1)} %add.55), dimensions={0} | broadcast | bytes 2377728 | tf_op jit(solution)/shard_map/broadcast_in_dim | solution.py:523
  75.5 40.3 %shard_map.83 = bf16[32,4608]{1,0:T(8,128)(2,1)} custom-call(bf16[4,256,1152]{2,1,0:T(8,128)(2,1)} %slice.25.got_ref, s32[4608,128]{1,0:T(8,128)} %broadcast_in_dim.21.key_ref, f32[1,4608]{1,0:T(1,128)} %precision_ref.1), custom_call_target="tpu_custom_call" | custom-call | tf_op jit(solution)/shard_map/pallas_call | solution.py:346
  115.9 4.9 %collective-permute-start = (bf16[32,4608]{1,0:T(8,128)(2,1)}, bf16[32,4608]{1,0:T(8,128)(2,1)S(1)}, u32[]{:S(2)}, u32[]{:S(2)}) collective-permute-start(bf16[32,4608]{1,0:T(8,128)(2,1)} %shard_map.83), channel_id=1, source_target_pairs={{1,0},{2,1},{3,2},{5,4},{6,5},{7,6},{9,8},{10,9},{11,10},{13,12},{... | collective-permute-start | bytes 884744 | tf_op jit(solution)/shard_map/ppermute | solution.py:16
  120.8 19.0 %shard_map.84 = f32[16,49,1]{2,1,0:T(8,128)} custom-call(s32[16]{0:T(128)} %broadcast_subtract_fusion.begin_ref, s32[16]{0:T(128)} %size_ref.3, bf16[16,49,4608]{2,1,0:T(8,128)(2,1)} %copy.22.weight_ref, bf16[64,10368]{1,0:T(8,128)(2,1)} %maximum_maximum_fusion.1.side_ref), custom_call_target="tpu_custom_call" | custom-call | flops 462422016 | bytes 7225344 | tf_op jit(solution)/shard_map/pallas_call | solution.py:425
  139.8 1.2 reduce.7
  141.1 10.1 %all_to_all.10 = f32[8,1,784]{2,1,0:T(1,128)S(1)} all-to-all(f32[8,1,784]{2,1,0:T(1,128)S(1)} %reshape.128), channel_id=1, replica_groups=mesh['cohort'=8,'stripe'=4] {'cohort'}, dimensions={0} | all-to-all | bytes 50176 | tf_op jit(solution)/shard_map/all_to_all | solution.py:509
  151.2 0.5 broadcast.178
  151.7 0.6 reduce.14
  152.5 1.1 copy.23.variance_ref
  153.6 1.0 maximum_maximum_fusion.2.side_ref
  154.6 18.9 %shard_map.85 = f32[16,49,32]{2,1,0:T(8,128)} custom-call(s32[16]{0:T(128)} %broadcast_subtract_fusion.begin_ref, s32[16]{0:T(128)} %size_ref.3, bf16[16,49,4608]{2,1,0:T(8,128)(2,1)} %copy.22.weight_ref, bf16[32,10368]{1,0:T(8,128)(2,1)} %maximum_maximum_fusion.2.side_ref, f32[16,49,1]{2,1,0:T(8,128)} %copy.23.variance_ref), custom_call_target="tpu_custom_call" | custom-call | flops 231211008 | bytes 7225344 | tf_op jit(solution)/shard_map/pallas_call | solution.py:425
  173.5 1.9 %copy.24 = f32[16,49,32]{1,2,0:T(8,128)} copy(f32[16,49,32]{2,1,0:T(8,128)} %shard_map.85) | data formatting | bytes 200704 | tf_op jit(solution)/shard_map/pallas_call | solution.py:425
  (32 shorter events, 1.3 us)
Async XLA Ops:
  1.1 50.1 %collective-permute-start.1 = (bf16[64,4608]{1,0:T(8,128)(2,1)S(1)}, bf16[64,4608]{1,0:T(8,128)(2,1)}, u32[]{:S(2)}, u32[]{:S(2)}) collective-permute-start(bf16[64,4608]{1,0:T(8,128)(2,1)S(1)} %constant_dynamic-slice_fusion), channel_id=1, source_target_pairs={{1,0},{2,1},{3,2},{5,4},{6,5},{7,6},{9,8},{10,9},{11,10},{13,12},{... | collective-permute-start | bytes 1769480 | tf_op jit(solution)/shard_map/ppermute | solution.py:16
  7.5 4.7 %copy-start.1 = (s32[1,4608]{1,0:T(1,128)S(1)}, s32[1,4608]{1,0:T(1,128)}, u32[]{:S(2)}) copy-start(s32[1,4608]{1,0:T(1,128)} %param.10) | copy-start | bytes 55300
  35.3 35.4 %all-to-all-start = ((bf16[4,272,1152]{2,1,0:T(8,128)(2,1)}), bf16[4,272,1152]{2,1,0:T(8,128)(2,1)S(1)}, u32[]{:S(2)}, u32[]{:S(2)}) async-start(bf16[4,272,1152]{2,1,0:T(8,128)(2,1)} %shard_map.82), calls=%async_computation | async-start | bytes 5013504 | tf_op jit(solution)/shard_map/all_to_all | solution.py:506
  40.5 10.2 %copy-start.2 = (s32[16]{0:T(128)S(1)}, s32[16]{0:T(128)}, u32[]{:S(2)}) copy-start(s32[16]{0:T(128)} %param.14) | copy-start | bytes 196
  115.9 37.7 %copy-start = (bf16[32,4608]{1,0:T(8,128)(2,1)S(1)}, bf16[32,4608]{1,0:T(8,128)(2,1)}, u32[]{:S(2)}) copy-start(bf16[32,4608]{1,0:T(8,128)(2,1)} %shard_map.83) | copy-start | bytes 884740
  115.9 37.7 %collective-permute-start = (bf16[32,4608]{1,0:T(8,128)(2,1)}, bf16[32,4608]{1,0:T(8,128)(2,1)S(1)}, u32[]{:S(2)}, u32[]{:S(2)}) collective-permute-start(bf16[32,4608]{1,0:T(8,128)(2,1)} %shard_map.83), channel_id=1, source_target_pairs={{1,0},{2,1},{3,2},{5,4},{6,5},{7,6},{9,8},{10,9},{11,10},{13,12},{... | collective-permute-start | bytes 884744 | tf_op jit(solution)/shard_map/ppermute | solution.py:16

commit v2 on v1

--- a/solution.py
+++ b/solution.py
@@ -152,16 +152,25 @@
 CHUNKS = 6
 
 
-def pack_kernel(low_ref, high_ref, left_ref, slot_ref, out_ref, total):
+def spread_column(row):
+    return jnp.transpose(jnp.broadcast_to(row, (128, 128)))
+
+
+def pack_kernel(low_ref, high_ref, left_ref, slot_ref, out_ref, total, column):
     block = pl.program_id(0)
     width = out_ref.shape[2]
     depth = left_ref.shape[1] // 4
     total[...] = jnp.zeros_like(total)
-    lane = lax.broadcasted_iota(jnp.int32, (depth, 128), 1) + block * width
+    lane = (lax.broadcasted_iota(jnp.int32, (depth, 128), 1) + block * width).astype(F32)
+
+    @pl.when(block == 0)
+    def _():
+        for b in range(slot_ref.shape[0]):
+            column[b * 128 : (b + 1) * 128, :] = spread_column(slot_ref[b : b + 1, :])
 
     def add_rows(k, carry):
         start = pl.multiple_of(k * depth, depth)
-        slots = slot_ref[pl.ds(start, depth), :]
+        slots = column[pl.ds(start, depth), :]
         chosen = jnp.concatenate(
             [
                 jnp.where(slots == lane + 128 * b, 1.0, 0.0).astype(BF16)
@@ -189,10 +198,10 @@
             grid=(stripes * 3,),
             in_specs=[
                 pl.BlockSpec((height, rows), lambda i, lo, hi: (0, 0)),
-                pl.BlockSpec((rows, 128), lambda i, lo, hi: (0, 0)),
+                pl.BlockSpec(slot.shape, lambda i, lo, hi: (0, 0)),
             ],
             out_specs=pl.BlockSpec((1, height, width), lambda i, lo, hi: (i // 3, 0, i % 3)),
-            scratch_shapes=[pltpu.VMEM((height, width), F32)],
+            scratch_shapes=[pltpu.VMEM((height, width), F32), pltpu.VMEM((rows, 128), F32)],
         ),
         out_shape=jax.ShapeDtypeStruct((stripes, height, bucket), BF16),
         cost_estimate=pl.CostEstimate(
@@ -203,10 +212,16 @@
 
 def combine_kernel(
     z_count,
+    traits,
     got_ref,
-    key_ref,
     precision_ref,
+    square_ref,
     out_ref,
+    variance_ref,
+    column,
+    mine,
+    rim,
+    squares,
     own,
     y_got,
     pair,
@@ -220,12 +235,18 @@
     z_recv,
     w_send,
     w_recv,
+    s_send,
+    s_recv,
+    r_send,
+    r_recv,
 ):
     cohort = lax.axis_index("cohort")
     stripe = lax.axis_index("stripe")
     cohorts = z_count * Y_COUNT
     z, y = cohort // Y_COUNT, lax.rem(cohort, Y_COUNT)
-    stripes, traits, bucket = got_ref.shape
+    stripes, _, bucket = got_ref.shape
+    rows = stripes * bucket
+    ahead, behind = lax.rem(stripe + 1, stripes), lax.rem(stripe + stripes - 1, stripes)
     block = traits // cohorts
     width = own.shape[4]
 
@@ -234,7 +255,9 @@
         pl.semaphore_signal(
             barrier, inc=1, device_id=(lax.rem(cohort + d, cohorts), stripe), device_id_type=MESH
         )
-    pl.semaphore_wait(barrier, cohorts - 1)
+    for other in (ahead, behind):
+        pl.semaphore_signal(barrier, inc=1, device_id=(cohort, other), device_id_type=MESH)
+    pl.semaphore_wait(barrier, cohorts + 1)
 
     def weight_copy(d):
         return pltpu.make_async_remote_copy(
@@ -243,6 +266,26 @@
             send_sem=w_send.at[d],
             recv_sem=w_recv.at[d],
             device_id=(lax.rem(cohort + d, cohorts), stripe),
+            device_id_type=MESH,
+        )
+
+    def square_copy(d):
+        return pltpu.make_async_remote_copy(
+            src_ref=square_ref,
+            dst_ref=squares.at[d],
+            send_sem=s_send.at[d],
+            recv_sem=s_recv.at[d],
+            device_id=(lax.rem(cohort + d, cohorts), stripe),
+            device_id_type=MESH,
+        )
+
+    def rim_copy(k):
+        return pltpu.make_async_remote_copy(
+            src_ref=mine.at[k],
+            dst_ref=rim.at[k],
+            send_sem=r_send.at[k],
+            recv_sem=r_recv.at[k],
+            device_id=(cohort, behind),
             device_id_type=MESH,
         )
 
@@ -269,16 +312,29 @@
 
     for d in range(1, cohorts):
         weight_copy(d).start()
+        square_copy(d).start()
     root[...] = jnp.sqrt(precision_ref[...])
+    out_ref[:, 2 * rows :] = jnp.zeros((block, out_ref.shape[1] - 2 * rows), BF16)
+
+    def spread_keys(s, carry):
+        digits = got_ref[s, traits : traits + 16, :].astype(F32)
+        keys = 64.0 * digits[0:1] + digits[1:2]
+        for b in range(bucket // 128):
+            column[pl.ds(pl.multiple_of(s * bucket + b * 128, 128), 128), :] = spread_column(
+                keys[:, b * 128 : (b + 1) * 128]
+            )
+        return carry
+
+    lax.fori_loop(0, stripes, spread_keys, 0)
 
     def step(k, carry):
         @pl.when(k < CHUNKS)
         def _():
-            lane = lax.broadcasted_iota(jnp.int32, (bucket, 128), 1) + k * width
+            lane = (lax.broadcasted_iota(jnp.int32, (bucket, 128), 1) + k * width).astype(F32)
             total[...] = jnp.zeros_like(total)
 
             def add_source(s, inner):
-                keys = key_ref[pl.ds(pl.multiple_of(s * bucket, bucket), bucket), :]
+                keys = column[pl.ds(pl.multiple_of(s * bucket, bucket), bucket), :]
                 chosen = jnp.concatenate(
                     [
                         jnp.where(keys == lane + 128 * b, 1.0, 0.0).astype(BF16)
@@ -286,7 +342,7 @@
                     ],
                     axis=1,
                 )
-                total[...] += jnp.dot(got_ref[s], chosen, preferred_element_type=F32)
+                total[...] += jnp.dot(got_ref[s, :traits, :], chosen, preferred_element_type=F32)
                 return inner
 
             lax.fori_loop(0, stripes, add_source, 0)
@@ -324,19 +380,36 @@
             z_copy(k, d).wait_recv()
             summed = summed + z_got[k, d].astype(F32)
         here = pl.ds(pl.multiple_of(k * width, width), width)
-        out_ref[:, here] = (summed / root[:, here]).astype(BF16)
+        value = (summed / root[:, here]).astype(BF16)
+        mine[k] = value
+        out_ref[:, here] = value
+        rim_copy(k).start()
         y_copy(k).wait_send()
         for d in range(1, z_count):
             z_copy(k, d).wait_send()
         return carry
 
     lax.fori_loop(0, CHUNKS, finish, 0)
+    square_sum = square_ref[...]
+    for d in range(1, cohorts):
+        square_copy(d).wait_recv()
+        square_sum = square_sum + squares[d]
+    variance_ref[...] = square_sum
+
+    def take_rim(k, carry):
+        rim_copy(k).wait_recv()
+        out_ref[:, pl.ds(pl.multiple_of(rows + k * width, width), width)] = rim[k]
+        rim_copy(k).wait_send()
+        return carry
+
+    lax.fori_loop(0, CHUNKS, take_rim, 0)
     for d in range(1, cohorts):
         weight_copy(d).wait_send()
-
-
-def combine(got, keys, precision, cohorts):
-    stripes, traits, bucket = got.shape
+        square_copy(d).wait_send()
+
+
+def combine(got, precision, squares, traits, cohorts, step):
+    stripes, _, bucket = got.shape
     rows = stripes * bucket
     width = rows // CHUNKS
     block = traits // cohorts
@@ -344,11 +417,18 @@
     vmem = pl.BlockSpec(memory_space=pltpu.VMEM)
     dma = pltpu.SemaphoreType.DMA
     return pl.pallas_call(
-        functools.partial(combine_kernel, z_count),
-        out_shape=jax.ShapeDtypeStruct((block, rows), BF16),
+        functools.partial(combine_kernel, z_count, traits),
+        out_shape=[
+            jax.ShapeDtypeStruct((block, 2 * rows + step), BF16),
+            jax.ShapeDtypeStruct(squares.shape, F32),
+        ],
         in_specs=[vmem] * 3,
-        out_specs=vmem,
+        out_specs=[vmem] * 2,
         scratch_shapes=[
+            pltpu.VMEM((rows, 128), F32),
+            pltpu.VMEM((CHUNKS, block, width), BF16),
+            pltpu.VMEM((CHUNKS, block, width), BF16),
+            pltpu.VMEM((cohorts,) + squares.shape, F32),
             pltpu.VMEM((CHUNKS, Y_COUNT, z_count, block, width), BF16),
             pltpu.VMEM((CHUNKS, z_count, block, width), BF16),
             pltpu.VMEM((CHUNKS, z_count, block, width), BF16),
@@ -362,83 +442,112 @@
             dma((CHUNKS, z_count)),
             dma((cohorts,)),
             dma((cohorts,)),
+            dma((cohorts,)),
+            dma((cohorts,)),
+            dma((CHUNKS,)),
+            dma((CHUNKS,)),
         ],
         compiler_params=pltpu.CompilerParams(collective_id=0, has_side_effects=True),
-    )(got, keys, precision)
-
-
-def window_product(begin, size, weight_ref, side_ref, total):
-    span = weight_ref.shape[2]
+    )(got, precision, squares)
+
+
+def variance_kernel(begin_ref, size_ref, weight_ref, side_ref, square_ref, aligned_ref, total):
+    group, tissues, span = weight_ref.shape
     step = span // 4
     blocks = step // 128
-    shift = lax.rem(begin, 128)
-    base = begin - shift
-    lane = lax.broadcasted_iota(jnp.int32, (weight_ref.shape[1], 128), 1)
-    total[...] = jnp.zeros_like(total)
-
-    def add_part(part, carry):
-        first = part * blocks
-
-        def turned(b):
-            at = jnp.clip(first + b, 0, span // 128 - 1)
-            piece = weight_ref[0, :, pl.ds(pl.multiple_of(at * 128, 128), 128)]
-            return pltpu.roll(piece.astype(F32), shift, 1)
-
-        before = turned(-1)
-        made = []
-        for b in range(blocks):
-            after = turned(b)
-            place = (first + b) * 128 + lane - shift
-            keep = jnp.logical_and(place >= 0, place < size)
-            made.append(
-                jnp.where(keep, jnp.where(lane < shift, before, after), 0.0).astype(BF16)
+    lane = lax.broadcasted_iota(jnp.int32, (tissues, 128), 1)
+
+    def one_gene(g, carry):
+        gene = pl.program_id(0) * group + g
+        size = size_ref[gene]
+        shift = lax.rem(begin_ref[gene], 128)
+        base = begin_ref[gene] - shift
+        total[...] = jnp.zeros_like(total)
+
+        def add_part(part, inner):
+            first = part * blocks
+
+            def turned(b):
+                at = jnp.clip(first + b, 0, span // 128 - 1)
+                piece = weight_ref[g, :, pl.ds(pl.multiple_of(at * 128, 128), 128)]
+                return pltpu.roll(piece.astype(F32), shift, 1)
+
+            before = turned(-1)
+            made = []
+            for b in range(blocks):
+                after = turned(b)
+                place = (first + b) * 128 + lane - shift
+                keep = jnp.logical_and(place >= 0, place < size)
+                made.append(
+                    jnp.where(keep, jnp.where(lane < shift, before, after), 0.0).astype(BF16)
+                )
+                before = after
+            made = jnp.concatenate(made, axis=1)
+            aligned_ref[g, :, pl.ds(pl.multiple_of(first * 128, 128), step)] = made
+            columns = side_ref[:, pl.ds(pl.multiple_of(base + first * 128, 128), step)]
+            total[...] += lax.dot_general(
+                columns, made, (((1,), (1,)), ((), ())), preferred_element_type=F32
             )
-            before = after
-        columns = side_ref[:, pl.ds(pl.multiple_of(base + first * 128, 128), step)]
-        total[...] += lax.dot_general(
-            jnp.concatenate(made, axis=1),
-            columns,
-            (((1,), (1,)), ((), ())),
-            preferred_element_type=F32,
-        )
+            return inner
+
+        lax.fori_loop(0, (size + shift + step - 1) // step, add_part, 0)
+        projected = total[...]
+        square_ref[g] = jnp.sum(projected * projected, axis=0, keepdims=True)
         return carry
 
-    lax.fori_loop(0, (size + shift + step - 1) // step, add_part, 0)
-
-
-def variance_kernel(begin_ref, size_ref, weight_ref, side_ref, out_ref, total):
-    gene = pl.program_id(0)
-    window_product(begin_ref[gene], size_ref[gene], weight_ref, side_ref, total)
-    projected = total[...]
-    out_ref[0] = jnp.sum(projected * projected, axis=1, keepdims=True)
-
-
-def score_kernel(begin_ref, size_ref, weight_ref, side_ref, variance_ref, out_ref, total):
-    gene = pl.program_id(0)
-    window_product(begin_ref[gene], size_ref[gene], weight_ref, side_ref, total)
-    out_ref[0] = total[...] / jnp.sqrt(variance_ref[0] + EPSILON)
-
-
-def by_gene(kernel, begin, size, weights, side, extra, width):
+    lax.fori_loop(0, group, one_gene, 0)
+
+
+def score_kernel(persons, begin_ref, size_ref, aligned_ref, side_ref, square_ref, out_ref, total):
+    group, tissues, span = aligned_ref.shape
+    step = span // 5
+
+    def one_gene(g, carry):
+        gene = pl.program_id(0) * group + g
+        shift = lax.rem(begin_ref[gene], 128)
+        base = begin_ref[gene] - shift
+        total[...] = jnp.zeros_like(total)
+
+        def add_part(part, inner):
+            first = part * step
+            total[...] += lax.dot_general(
+                side_ref[:, pl.ds(pl.multiple_of(base + first, 128), step)],
+                aligned_ref[g, :, pl.ds(pl.multiple_of(first, 128), step)],
+                (((1,), (1,)), ((), ())),
+                preferred_element_type=F32,
+            )
+            return inner
+
+        lax.fori_loop(0, (size_ref[gene] + shift + step - 1) // step, add_part, 0)
+        out_ref[g] = total[...] / jnp.sqrt(square_ref[g] / persons + EPSILON)
+        return carry
+
+    lax.fori_loop(0, group, one_gene, 0)
+
+
+def by_gene(kernel, begin, size, weights, side, extra, outs, group):
     genes, tissues, span = weights.shape
-    column = pl.BlockSpec((1, tissues, 1), lambda g, b, s: (g, 0, 0))
+
+    def rows_of(shape):
+        return pl.BlockSpec((group,) + shape[1:], lambda g, b, s: (g, 0, 0))
+
     return pl.pallas_call(
         kernel,
         grid_spec=pltpu.PrefetchScalarGridSpec(
             num_scalar_prefetch=2,
-            grid=(genes,),
+            grid=(genes // group,),
             in_specs=[
-                pl.BlockSpec((1, tissues, span), lambda g, b, s: (g, 0, 0)),
+                rows_of(weights.shape),
                 pl.BlockSpec(side.shape, lambda g, b, s: (0, 0)),
             ]
-            + [column] * len(extra),
-            out_specs=pl.BlockSpec((1, tissues, width), lambda g, b, s: (g, 0, 0)),
-            scratch_shapes=[pltpu.VMEM((tissues, side.shape[0]), F32)],
+            + [rows_of(e.shape) for e in extra],
+            out_specs=[rows_of(o.shape) for o in outs],
+            scratch_shapes=[pltpu.VMEM((side.shape[0], tissues), F32)],
         ),
-        out_shape=jax.ShapeDtypeStruct((genes, tissues, width), F32),
+        out_shape=outs,
         cost_estimate=pl.CostEstimate(
-            flops=2 * genes * tissues * span * side.shape[0],
-            bytes_accessed=2 * genes * tissues * span,
+            flops=16 * genes * tissues * span * side.shape[0],
+            bytes_accessed=4 * genes * tissues * span,
             transcendentals=0,
         ),
     )(begin, size, weights, side, *extra)
@@ -498,42 +607,40 @@
     )
     outgoing = pack_rows(
         left,
-        jnp.broadcast_to(slot[:, None], (row_count, 128)),
+        slot.reshape(row_count // 128, 128).astype(F32),
         low.reshape(-1),
         high.reshape(-1),
         stripes,
     )
     got = lax.all_to_all(outgoing, "stripe", split_axis=0, concat_axis=0, tiled=True)
 
-    squares = by_gene(variance_kernel, begin, window_length, gene_weights, panel_ext, (), 1)
-    shares = lax.all_to_all(
-        jnp.broadcast_to(squares[:, :, 0][None], (cohorts,) + squares.shape[:2]),
-        "cohort",
-        split_axis=0,
-        concat_axis=0,
-        tiled=True,
-    )
-    variance = jnp.sum(shares, axis=0)[:, :, None] / persons
-
-    keys = (
-        64 * got[:, trait_count].astype(jnp.int32) + got[:, trait_count + 1].astype(jnp.int32)
-    ).reshape(row_count)
-    combined = combine(
-        got[:, :trait_count],
-        jnp.broadcast_to(keys[:, None], (row_count, 128)),
-        precision,
-        cohorts,
-    )
-    score_ext = extended(combined, step)
-    return by_gene(
-        score_kernel,
+    genes, tissues, _ = gene_weights.shape
+    group = 4 if genes % 4 == 0 else 1
+    squares, aligned = by_gene(
+        variance_kernel,
         begin,
         window_length,
         gene_weights,
+        panel_ext,
+        (),
+        [
+            jax.ShapeDtypeStruct((genes, 1, tissues), F32),
+            jax.ShapeDtypeStruct((genes, tissues, 5 * step), BF16),
+        ],
+        group,
+    )
+    score_ext, square_sums = combine(got, precision, squares, trait_count, cohorts, step)
+    (association,) = by_gene(
+        functools.partial(score_kernel, persons),
+        begin,
+        window_length,
+        aligned,
         score_ext,
-        (variance,),
-        combined.shape[0],
-    )
+        (square_sums,),
+        [jax.ShapeDtypeStruct((genes, score_ext.shape[0], tissues), F32)],
+        group,
+    )
+    return jnp.transpose(association, (0, 2, 1))
 
 
 def on_device(cohort_scores, *others):

time: 177 us -> 131 us (0.74)
  waiting for transfers between devices: 17.1 us -> 1.82 us
  blocking collectives: 10.1 us -> 0 us
  local copies, waits for them, and re-layouts: 27.6 us -> 17.7 us
  starting transfers between devices: 12 us -> 7.07 us
  Pallas kernels: 95.9 us -> 91.3 us
  other arithmetic: 12.6 us -> 10.2 us
    all_to_all x1, waiting for transfers between devices: 17.1 us -> 1.81 us  [fast_device(): lax.all_to_all(outgoing, 'stripe', split_axis=0, concat_axis=0, tiled=True)]
    pallas_call x2, Pallas kernels: 37.9 us -> 26.4 us  [by_gene(): pl.pallas_call(kernel, grid_spec=pltpu.PrefetchScalarGridSpec(num_scalar_...]
    all_to_all x1 -> x0, blocking collectives: 10.1 us -> none  [fast_device(): lax.all_to_all(jnp.broadcast_to(squares[:, :, 0][None], (cohorts,) + squa...]
    pallas_call x1, Pallas kernels: 40.3 us -> 47.3 us  [combine(): pl.pallas_call(functools.partial(combine_kernel, z_count, traits), out_sh...]
    broadcast_in_dim x3 -> x0, local copies, waits for them, and re-layouts: 6.19 us -> none  [the longest x1 3.1 us: fast_device(): jnp.broadcast_to(slot[:, None], (row_count, 128))]
    ppermute x2 -> x1, starting transfers between devices: 6.81 us -> 1.93 us  [passed_along(): return lax.ppermute(block, axis, route)]
    pallas_call x1 -> x0, local copies, waits for them, and re-layouts: 1.92 us -> none  [by_gene(): pl.pallas_call(kernel, grid_spec=pltpu.PrefetchScalarGridSpec(num_scalar_...]
    unnamed x11 -> x9, local copies, waits for them, and re-layouts: 13.3 us -> 14.7 us
  transfers between devices with their start and end apart: 3 -> 2, of which waited for: 1 -> 1; matrix products, arithmetic and copies ran while one was open for 18% -> 20% of each run, Pallas kernels for 21% -> 26%
where the time goes in v2:
time: 131 us; the launch traced here: 128 us
  Pallas kernels  91.3 us (70%)
  local copies, waits for them, and re-layouts  17.7 us (14%)
  other arithmetic  10.2 us (8%)
  starting transfers between devices  7.07 us (5%)
  waiting for transfers between devices  1.82 us (1%)
    pallas_call x1, Pallas kernels, combine(): pl.pallas_call(functools.partial(combine_kernel, z_count, traits), out_sh...  47.3 us
    pallas_call x2, Pallas kernels, by_gene(): pl.pallas_call(kernel, grid_spec=pltpu.PrefetchScalarGridSpec(num_scalar_...  26.4 us
    pallas_call x1, Pallas kernels, pack_rows(): pl.pallas_call(pack_kernel, grid_spec=pltpu.PrefetchScalarGridSpec(num_sc...  17.6 us
    unnamed x9, local copies, waits for them, and re-layouts  14.7 us
    all_to_all x1, starting transfers between devices, fast_device(): lax.all_to_all(outgoing, 'stripe', split_axis=0, concat_axis=0, tiled=True)  5.15 us
  transfers between devices with their start and end apart: 2, of which 1 were waited for; matrix products, arithmetic and copies ran while one was open for 20% of the time, Pallas kernels for 26%

profile of v2, /device:TPU:1, one launch (start us, length us, event | category | flops | bytes accessed | tf_op | source)
XLA Modules:
  0.0 128.2 jit_solution(14562653974186754982)
XLA Ops:
  0.0 1.1 constant_dynamic-slice_fusion
  1.1 1.9 %collective-permute-start = (bf16[64,4608]{1,0:T(8,128)(2,1)S(1)}, bf16[64,4608]{1,0:T(8,128)(2,1)}, u32[]{:S(2)}, u32[]{:S(2)}) collective-permute-start(bf16[64,4608]{1,0:T(8,128)(2,1)S(1)} %constant_dynamic-slice_fusion), channel_id=1, source_target_pairs={{1,0},{2,1},{3,2},{5,4},{6,5},{7,6},{9,8},{10,9},{11,10},{13,12},{... | collective-permute-start | bytes 1769480 | tf_op jit(solution)/shard_map/ppermute | solution.py:16
  3.1 0.9 fusion.5
  4.0 0.9 fusion.7
  4.8 0.9 fusion.8
  5.8 1.2 reduce-window.6
  6.9 0.2 slice_reduce_fusion
  7.2 0.2 reduce-window.9
  7.4 0.1 select_reduce_fusion
  7.5 0.0 copy-start.1
  7.5 0.1 slice.11
  7.6 0.2 convert_reduce_fusion.1
  7.9 0.1 copy.14
  8.0 0.7 reshape.68.low_ref
  8.6 0.1 copy.15
  8.7 0.7 add.33.high_ref
  9.4 2.8 %copy.16 = bf16[1,4608,256]{1,2,0:T(8,128)(2,1)S(1)} copy(bf16[1,4608,256]{2,1,0:T(8,128)(2,1)} %param.8) | data formatting | bytes 4718592 | tf_op args[0]
  12.3 0.1 convert_reduce_fusion
  12.4 0.2 fusion
  12.5 0.1 pad.3.clone
  12.6 0.6 fusion.4.slot_ref
  13.2 2.0 %maximum_maximum_fusion.left_ref = bf16[272,4608]{1,0:T(8,128)(2,1)} fusion(bf16[1,4608]{1,0:T(2,128)(2,1)S(1)} %convert_element_type.37, bf16[1,4608]{1,0:T(2,128)(2,1)S(1)} %get-tuple-element.17, bf16[256,4608]{1,0:T(8,128)(2,1)S(1)} %fusion, bf16[272]{0:T(512)(128)(2,1)S(1)} %pad.3.clone), kind=kLoop, calls=%fused_computation | loop fusion | flops 10027008 | bytes 4885024 | tf_op jit(solution)/shard_map/concatenate | solution.py:599
  15.3 17.6 %shard_map.83 = bf16[4,272,1152]{2,1,0:T(8,128)(2,1)} custom-call(s32[12]{0:T(128)} %reshape.68.low_ref, s32[12]{0:T(128)} %add.33.high_ref, bf16[272,4608]{1,0:T(8,128)(2,1)} %maximum_maximum_fusion.left_ref, f32[36,128]{1,0:T(8,128)} %fusion.4.slot_ref), custom_call_target="tpu_custom_call" | custom-call | flops 5775556608 | bytes 5013504 | tf_op jit(solution)/shard_map/pallas_call | solution.py:194
  32.9 5.1 %all-to-all-start = ((bf16[4,272,1152]{2,1,0:T(8,128)(2,1)}), bf16[4,272,1152]{2,1,0:T(8,128)(2,1)S(1)}, u32[]{:S(2)}, u32[]{:S(2)}) async-start(bf16[4,272,1152]{2,1,0:T(8,128)(2,1)} %shard_map.83), calls=%async_computation | async-start | bytes 5013504 | tf_op jit(solution)/shard_map/all_to_all | solution.py:615
  38.0 10.3 %copy.13.weight_ref = bf16[16,49,4608]{2,1,0:T(8,128)(2,1)} copy(bf16[16,49,4608]{2,0,1:T(8,128)(2,1)} %param.13) | data formatting | bytes 14450688 | tf_op args[5]
  48.4 0.5 broadcast_subtract_fusion.begin_ref
  48.9 2.3 %maximum_maximum_fusion.1.side_ref = bf16[64,10368]{1,0:T(8,128)(2,1)} fusion(bf16[64,4608]{1,0:T(8,128)(2,1)} %collective-permute-done, bf16[64,4608]{1,0:T(8,128)(2,1)S(1)} %constant_dynamic-slice_fusion, bf16[10368]{0:T(1024)(128)(2,1)S(1)} %pad.6.clone), kind=kLoop, calls=%fused_computation.3 | loop fusion | flops 3981312 | bytes 2527488 | tf_op jit(solution)/shard_map/concatenate | solution.py:558
  51.2 15.2 %shard_map.82 = (f32[16,1,49]{2,1,0:T(1,128)}, bf16[16,49,5760]{2,1,0:T(8,128)(2,1)}) custom-call(s32[16]{0:T(128)} %broadcast_subtract_fusion.begin_ref, s32[16]{0:T(128)} %size_ref.3, bf16[16,49,4608]{2,1,0:T(8,128)(2,1)} %copy.13.weight_ref, bf16[64,10368]{1,0:T(8,128)(2,1)} %maximum_maximum_fusion.1.side_ref), custom_call_target="tpu_custom_call" | custom-call | flops 3699376128 | bytes 14450688 | tf_op jit(solution)/shard_map/pallas_call | solution.py:534
  66.4 1.8 %all-to-all-done.got_ref = bf16[4,272,1152]{2,1,0:T(8,128)(2,1)S(1)} async-done(((bf16[4,272,1152]{2,1,0:T(8,128)(2,1)}), bf16[4,272,1152]{2,1,0:T(8,128)(2,1)S(1)}, u32[]{:S(2)}, u32[]{:S(2)}) %all-to-all-start) | async-done | bytes 2506784 | tf_op jit(solution)/shard_map/all_to_all | solution.py:615
  68.2 1.5 %copy-done = bf16[4,272,1152]{2,1,0:T(8,128)(2,1)} copy-done((bf16[4,272,1152]{2,1,0:T(8,128)(2,1)}, bf16[4,272,1152]{2,1,0:T(8,128)(2,1)S(1)}, u32[]{:S(2)}) %copy-start) | copy-done | bytes 2506776
  69.7 47.3 %shard_map.84 = (bf16[32,10368]{1,0:T(8,128)(2,1)}, f32[16,1,49]{2,1,0:T(1,128)}) custom-call(bf16[4,272,1152]{2,1,0:T(8,128)(2,1)} %copy-done, f32[1,4608]{1,0:T(1,128)} %precision_ref.1, f32[16,1,49]{2,1,0:T(1,128)} %get-tuple-element.10.square_ref), custom_call_target="tpu_custom_call" | custom-call | tf_op jit(solution)/shard_map/pallas_call | solution.py:419
  117.0 11.2 %shard_map.85 = f32[16,32,49]{2,1,0:T(8,128)} custom-call(s32[16]{0:T(128)} %broadcast_subtract_fusion.begin_ref, s32[16]{0:T(128)} %size_ref.3, bf16[16,49,5760]{2,1,0:T(8,128)(2,1)} %get-tuple-element.9.aligned_ref, bf16[32,10368]{1,0:T(8,128)(2,1)} %get-tuple-element.11.side_ref, f32[16,1,49]{2,1,0:T(1,128)} %get-tuple-element.12.square_ref), custom_call_target="tpu_custom_call" | custom-call | flops 2312110080 | bytes 18063360 | tf_op jit(solution)/shard_map/pallas_call | solution.py:534
  (13 shorter events, 0.1 us)
Async XLA Ops:
  1.1 47.8 %collective-permute-start = (bf16[64,4608]{1,0:T(8,128)(2,1)S(1)}, bf16[64,4608]{1,0:T(8,128)(2,1)}, u32[]{:S(2)}, u32[]{:S(2)}) collective-permute-start(bf16[64,4608]{1,0:T(8,128)(2,1)S(1)} %constant_dynamic-slice_fusion), channel_id=1, source_target_pairs={{1,0},{2,1},{3,2},{5,4},{6,5},{7,6},{9,8},{10,9},{11,10},{13,12},{... | collective-permute-start | bytes 1769480 | tf_op jit(solution)/shard_map/ppermute | solution.py:16
  7.5 4.8 %copy-start.1 = (s32[1,4608]{1,0:T(1,128)S(1)}, s32[1,4608]{1,0:T(1,128)}, u32[]{:S(2)}) copy-start(s32[1,4608]{1,0:T(1,128)} %param.10) | copy-start | bytes 55300
  32.9 35.4 %all-to-all-start = ((bf16[4,272,1152]{2,1,0:T(8,128)(2,1)}), bf16[4,272,1152]{2,1,0:T(8,128)(2,1)S(1)}, u32[]{:S(2)}, u32[]{:S(2)}) async-start(bf16[4,272,1152]{2,1,0:T(8,128)(2,1)} %shard_map.83), calls=%async_computation | async-start | bytes 5013504 | tf_op jit(solution)/shard_map/all_to_all | solution.py:615
  38.0 10.3 %copy-start.2 = (s32[16]{0:T(128)S(1)}, s32[16]{0:T(128)}, u32[]{:S(2)}) copy-start(s32[16]{0:T(128)} %param.14) | copy-start | bytes 196
  68.2 1.5 %copy-start = (bf16[4,272,1152]{2,1,0:T(8,128)(2,1)}, bf16[4,272,1152]{2,1,0:T(8,128)(2,1)S(1)}, u32[]{:S(2)}) copy-start(bf16[4,272,1152]{2,1,0:T(8,128)(2,1)S(1)} %all-to-all-done.got_ref) | copy-start | bytes 7520260

commit v3 on v2

--- a/solution.py
+++ b/solution.py
@@ -149,7 +149,7 @@
 BF16 = jnp.bfloat16
 F32 = jnp.float32
 Y_COUNT = 2
-CHUNKS = 6
+CHUNKS = 9
 
 
 def spread_column(row):
@@ -159,7 +159,7 @@
 def pack_kernel(low_ref, high_ref, left_ref, slot_ref, out_ref, total, column):
     block = pl.program_id(0)
     width = out_ref.shape[2]
-    depth = left_ref.shape[1] // 4
+    depth = left_ref.shape[1] // 6
     total[...] = jnp.zeros_like(total)
     lane = (lax.broadcasted_iota(jnp.int32, (depth, 128), 1) + block * width).astype(F32)
 
@@ -330,11 +330,11 @@
     def step(k, carry):
         @pl.when(k < CHUNKS)
         def _():
-            lane = (lax.broadcasted_iota(jnp.int32, (bucket, 128), 1) + k * width).astype(F32)
+            lane = (lax.broadcasted_iota(jnp.int32, (2 * bucket, 128), 1) + k * width).astype(F32)
             total[...] = jnp.zeros_like(total)
 
             def add_source(s, inner):
-                keys = column[pl.ds(pl.multiple_of(s * bucket, bucket), bucket), :]
+                keys = column[pl.ds(pl.multiple_of(2 * s * bucket, 2 * bucket), 2 * bucket), :]
                 chosen = jnp.concatenate(
                     [
                         jnp.where(keys == lane + 128 * b, 1.0, 0.0).astype(BF16)
@@ -342,10 +342,13 @@
                     ],
                     axis=1,
                 )
-                total[...] += jnp.dot(got_ref[s, :traits, :], chosen, preferred_element_type=F32)
+                both = jnp.concatenate(
+                    [got_ref[2 * s, :traits, :], got_ref[2 * s + 1, :traits, :]], axis=1
+                )
+                total[...] += jnp.dot(both, chosen, preferred_element_type=F32)
                 return inner
 
-            lax.fori_loop(0, stripes, add_source, 0)
+            lax.fori_loop(0, stripes // 2, add_source, 0)
             scale = root[:, pl.ds(pl.multiple_of(k * width, width), width)]
             for c in range(cohorts):
                 own[k, c % Y_COUNT, c // Y_COUNT] = (
@@ -590,7 +593,7 @@
     rank = jnp.sum(jnp.where(member, ranking, 0), axis=0) - 1
     slot = target * bucket + rank
     width = bucket // 3
-    depth = row_count // 4
+    depth = row_count // 6
     ends = ranking[:, depth - 1 :: depth]
     edges = jnp.arange(3, dtype=jnp.int32) * width
     low = jnp.sum(ends[:, None, :] <= edges[None, :, None], axis=2, dtype=jnp.int32)
@@ -653,6 +656,8 @@
         and traits % (16 * cohorts) == 0
         and rows % (384 * stripes) == 0
         and rows % (128 * CHUNKS) == 0
+        and rows % 768 == 0
+        and stripes % 2 == 0
         and rows < 16384
         and span % 512 == 0
         and span <= rows

time: 131 us -> 131 us (level); the launches traced: 128 us -> 130 us
  Pallas kernels: 91.3 us -> 94.7 us
  waiting for transfers between devices: 1.82 us -> 0.01 us
    pallas_call x2, Pallas kernels: 26.4 us -> 30.2 us  [by_gene(): pl.pallas_call(kernel, grid_spec=pltpu.PrefetchScalarGridSpec(num_scalar_...]
    all_to_all x1, waiting for transfers between devices: 1.81 us -> 0.01 us  [fast_device(): lax.all_to_all(outgoing, 'stripe', split_axis=0, concat_axis=0, tiled=True)]
  transfers between devices with their start and end apart: 2 -> 2, of which waited for: 1 -> 0; matrix products, arithmetic and copies ran while one was open for 20% -> 20% of each run, Pallas kernels for 26% -> 27%
where the time goes in v3:
time: 131 us; the launch traced here: 130 us
  Pallas kernels  94.7 us (72%)
  local copies, waits for them, and re-layouts  17.7 us (14%)
  other arithmetic  10.2 us (8%)
  starting transfers between devices  7.1 us (5%)
    pallas_call x1, Pallas kernels, combine(): pl.pallas_call(functools.partial(combine_kernel, z_count, traits), out_sh...  47.2 us
    pallas_call x2, Pallas kernels, by_gene(): pl.pallas_call(kernel, grid_spec=pltpu.PrefetchScalarGridSpec(num_scalar_...  30.2 us
    pallas_call x1, Pallas kernels, pack_rows(): pl.pallas_call(pack_kernel, grid_spec=pltpu.PrefetchScalarGridSpec(num_sc...  17.2 us
    unnamed x9, local copies, waits for them, and re-layouts  14.7 us
    all_to_all x1, starting transfers between devices, fast_device(): lax.all_to_all(outgoing, 'stripe', split_axis=0, concat_axis=0, tiled=True)  5.17 us
  transfers between devices with their start and end apart: 2, of which 0 were waited for; matrix products, arithmetic and copies ran while one was open for 20% of the time, Pallas kernels for 27%

profile of v3, /device:TPU:1, one launch (start us, length us, event | category | flops | bytes accessed | tf_op | source)
XLA Modules:
  0.0 129.8 jit_solution(10331553921707340477)
XLA Ops:
  0.0 1.1 constant_dynamic-slice_fusion
  1.1 1.9 %collective-permute-start = (bf16[64,4608]{1,0:T(8,128)(2,1)S(1)}, bf16[64,4608]{1,0:T(8,128)(2,1)}, u32[]{:S(2)}, u32[]{:S(2)}) collective-permute-start(bf16[64,4608]{1,0:T(8,128)(2,1)S(1)} %constant_dynamic-slice_fusion), channel_id=1, source_target_pairs={{1,0},{2,1},{3,2},{5,4},{6,5},{7,6},{9,8},{10,9},{11,10},{13,12},{... | collective-permute-start | bytes 1769480 | tf_op jit(solution)/shard_map/ppermute | solution.py:16
  3.1 0.9 fusion.5
  4.0 0.9 fusion.7
  4.8 0.9 fusion.8
  5.8 1.2 reduce-window.6
  6.9 0.2 slice_reduce_fusion
  7.2 0.2 reduce-window.9
  7.4 0.1 select_reduce_fusion
  7.5 0.0 copy-start.1
  7.5 0.1 slice.11
  7.6 0.2 convert_reduce_fusion.1
  7.9 0.1 copy.14
  8.0 0.7 reshape.68.low_ref
  8.6 0.1 copy.15
  8.7 0.7 add.33.high_ref
  9.4 2.8 %copy.16 = bf16[1,4608,256]{1,2,0:T(8,128)(2,1)S(1)} copy(bf16[1,4608,256]{2,1,0:T(8,128)(2,1)} %param.8) | data formatting | bytes 4718592 | tf_op args[0]
  12.3 0.1 convert_reduce_fusion
  12.4 0.2 fusion
  12.5 0.1 pad.3.clone
  12.6 0.6 fusion.4.slot_ref
  13.2 2.0 %maximum_maximum_fusion.left_ref = bf16[272,4608]{1,0:T(8,128)(2,1)} fusion(bf16[1,4608]{1,0:T(2,128)(2,1)S(1)} %convert_element_type.37, bf16[1,4608]{1,0:T(2,128)(2,1)S(1)} %get-tuple-element.17, bf16[256,4608]{1,0:T(8,128)(2,1)S(1)} %fusion, bf16[272]{0:T(512)(128)(2,1)S(1)} %pad.3.clone), kind=kLoop, calls=%fused_computation | loop fusion | flops 10027008 | bytes 4885024 | tf_op jit(solution)/shard_map/concatenate | solution.py:602
  15.3 17.2 %shard_map.83 = bf16[4,272,1152]{2,1,0:T(8,128)(2,1)} custom-call(s32[12]{0:T(128)} %reshape.68.low_ref, s32[12]{0:T(128)} %add.33.high_ref, bf16[272,4608]{1,0:T(8,128)(2,1)} %maximum_maximum_fusion.left_ref, f32[36,128]{1,0:T(8,128)} %fusion.4.slot_ref), custom_call_target="tpu_custom_call" | custom-call | flops 5775556608 | bytes 5013504 | tf_op jit(solution)/shard_map/pallas_call | solution.py:194
  32.5 5.2 %all-to-all-start = ((bf16[4,272,1152]{2,1,0:T(8,128)(2,1)}), bf16[4,272,1152]{2,1,0:T(8,128)(2,1)S(1)}, u32[]{:S(2)}, u32[]{:S(2)}) async-start(bf16[4,272,1152]{2,1,0:T(8,128)(2,1)} %shard_map.83), calls=%async_computation | async-start | bytes 5013504 | tf_op jit(solution)/shard_map/all_to_all | solution.py:618
  37.7 10.3 %copy.13.weight_ref = bf16[16,49,4608]{2,1,0:T(8,128)(2,1)} copy(bf16[16,49,4608]{2,0,1:T(8,128)(2,1)} %param.13) | data formatting | bytes 14450688 | tf_op args[5]
  48.0 0.5 broadcast_subtract_fusion.begin_ref
  48.5 2.3 %maximum_maximum_fusion.1.side_ref = bf16[64,10368]{1,0:T(8,128)(2,1)} fusion(bf16[64,4608]{1,0:T(8,128)(2,1)} %collective-permute-done, bf16[64,4608]{1,0:T(8,128)(2,1)S(1)} %constant_dynamic-slice_fusion, bf16[10368]{0:T(1024)(128)(2,1)S(1)} %pad.6.clone), kind=kLoop, calls=%fused_computation.3 | loop fusion | flops 3981312 | bytes 2527488 | tf_op jit(solution)/shard_map/concatenate | solution.py:561
  50.9 17.6 %shard_map.82 = (f32[16,1,49]{2,1,0:T(1,128)}, bf16[16,49,5760]{2,1,0:T(8,128)(2,1)}) custom-call(s32[16]{0:T(128)} %broadcast_subtract_fusion.begin_ref, s32[16]{0:T(128)} %size_ref.3, bf16[16,49,4608]{2,1,0:T(8,128)(2,1)} %copy.13.weight_ref, bf16[64,10368]{1,0:T(8,128)(2,1)} %maximum_maximum_fusion.1.side_ref), custom_call_target="tpu_custom_call" | custom-call | flops 3699376128 | bytes 14450688 | tf_op jit(solution)/shard_map/pallas_call | solution.py:537
  68.4 0.0 all-to-all-done.got_ref
  68.4 1.5 %copy-done = bf16[4,272,1152]{2,1,0:T(8,128)(2,1)} copy-done((bf16[4,272,1152]{2,1,0:T(8,128)(2,1)}, bf16[4,272,1152]{2,1,0:T(8,128)(2,1)S(1)}, u32[]{:S(2)}) %copy-start) | copy-done | bytes 2506776
  69.9 47.2 %shard_map.84 = (bf16[32,10368]{1,0:T(8,128)(2,1)}, f32[16,1,49]{2,1,0:T(1,128)}) custom-call(bf16[4,272,1152]{2,1,0:T(8,128)(2,1)} %copy-done, f32[1,4608]{1,0:T(1,128)} %precision_ref.1, f32[16,1,49]{2,1,0:T(1,128)} %get-tuple-element.10.square_ref), custom_call_target="tpu_custom_call" | custom-call | tf_op jit(solution)/shard_map/pallas_call | solution.py:422
  117.1 12.7 %shard_map.85 = f32[16,32,49]{2,1,0:T(8,128)} custom-call(s32[16]{0:T(128)} %broadcast_subtract_fusion.begin_ref, s32[16]{0:T(128)} %size_ref.3, bf16[16,49,5760]{2,1,0:T(8,128)(2,1)} %get-tuple-element.9.aligned_ref, bf16[32,10368]{1,0:T(8,128)(2,1)} %get-tuple-element.11.side_ref, f32[16,1,49]{2,1,0:T(1,128)} %get-tuple-element.12.square_ref), custom_call_target="tpu_custom_call" | custom-call | flops 2312110080 | bytes 18063360 | tf_op jit(solution)/shard_map/pallas_call | solution.py:537
  (13 shorter events, 0.1 us)
Async XLA Ops:
  1.1 47.4 %collective-permute-start = (bf16[64,4608]{1,0:T(8,128)(2,1)S(1)}, bf16[64,4608]{1,0:T(8,128)(2,1)}, u32[]{:S(2)}, u32[]{:S(2)}) collective-permute-start(bf16[64,4608]{1,0:T(8,128)(2,1)S(1)} %constant_dynamic-slice_fusion), channel_id=1, source_target_pairs={{1,0},{2,1},{3,2},{5,4},{6,5},{7,6},{9,8},{10,9},{11,10},{13,12},{... | collective-permute-start | bytes 1769480 | tf_op jit(solution)/shard_map/ppermute | solution.py:16
  7.5 4.8 %copy-start.1 = (s32[1,4608]{1,0:T(1,128)S(1)}, s32[1,4608]{1,0:T(1,128)}, u32[]{:S(2)}) copy-start(s32[1,4608]{1,0:T(1,128)} %param.10) | copy-start | bytes 55300
  32.5 35.9 %all-to-all-start = ((bf16[4,272,1152]{2,1,0:T(8,128)(2,1)}), bf16[4,272,1152]{2,1,0:T(8,128)(2,1)S(1)}, u32[]{:S(2)}, u32[]{:S(2)}) async-start(bf16[4,272,1152]{2,1,0:T(8,128)(2,1)} %shard_map.83), calls=%async_computation | async-start | bytes 5013504 | tf_op jit(solution)/shard_map/all_to_all | solution.py:618
  37.7 10.3 %copy-start.2 = (s32[16]{0:T(128)S(1)}, s32[16]{0:T(128)}, u32[]{:S(2)}) copy-start(s32[16]{0:T(128)} %param.14) | copy-start | bytes 196
  68.4 1.5 %copy-start = (bf16[4,272,1152]{2,1,0:T(8,128)(2,1)}, bf16[4,272,1152]{2,1,0:T(8,128)(2,1)S(1)}, u32[]{:S(2)}) copy-start(bf16[4,272,1152]{2,1,0:T(8,128)(2,1)S(1)} %all-to-all-done.got_ref) | copy-start | bytes 7520260

commit v4 on v3

--- a/solution.py
+++ b/solution.py
@@ -152,6 +152,9 @@
 CHUNKS = 9
 
 
+LAG = 4
+
+
 def spread_column(row):
     return jnp.transpose(jnp.broadcast_to(row, (128, 128)))
 
@@ -228,6 +231,7 @@
     z_got,
     weights,
     root,
+    norm,
     total,
     y_send,
     y_recv,
@@ -356,7 +360,7 @@
                 ).astype(BF16)
             y_copy(k).start()
 
-        @pl.when(k >= 1)
+        @pl.when(jnp.logical_and(k >= 1, k <= CHUNKS))
         def _():
             last = k - 1
             y_copy(last).wait_recv()
@@ -367,32 +371,33 @@
             for d in range(1, z_count):
                 z_copy(last, d).start()
 
+        @pl.when(k == LAG)
+        def _():
+            weight_sum = precision_ref[...]
+            for d in range(1, cohorts):
+                weight_copy(d).wait_recv()
+                weight_sum = weight_sum + weights[d]
+            norm[...] = jnp.sqrt(weight_sum)
+
+        @pl.when(k >= LAG)
+        def _():
+            done = k - LAG
+            summed = pair[done, z].astype(F32)
+            for d in range(1, z_count):
+                z_copy(done, d).wait_recv()
+                summed = summed + z_got[done, d].astype(F32)
+            here = pl.ds(pl.multiple_of(done * width, width), width)
+            value = (summed / norm[:, here]).astype(BF16)
+            mine[done] = value
+            out_ref[:, here] = value
+            rim_copy(done).start()
+            y_copy(done).wait_send()
+            for d in range(1, z_count):
+                z_copy(done, d).wait_send()
+
         return carry
 
-    lax.fori_loop(0, CHUNKS + 1, step, 0)
-
-    weight_sum = precision_ref[...]
-    for d in range(1, cohorts):
-        weight_copy(d).wait_recv()
-        weight_sum = weight_sum + weights[d]
-    root[...] = jnp.sqrt(weight_sum)
-
-    def finish(k, carry):
-        summed = pair[k, z].astype(F32)
-        for d in range(1, z_count):
-            z_copy(k, d).wait_recv()
-            summed = summed + z_got[k, d].astype(F32)
-        here = pl.ds(pl.multiple_of(k * width, width), width)
-        value = (summed / root[:, here]).astype(BF16)
-        mine[k] = value
-        out_ref[:, here] = value
-        rim_copy(k).start()
-        y_copy(k).wait_send()
-        for d in range(1, z_count):
-            z_copy(k, d).wait_send()
-        return carry
-
-    lax.fori_loop(0, CHUNKS, finish, 0)
+    lax.fori_loop(0, CHUNKS + LAG, step, 0)
     square_sum = square_ref[...]
     for d in range(1, cohorts):
         square_copy(d).wait_recv()
@@ -438,6 +443,7 @@
             pltpu.VMEM((CHUNKS, z_count, block, width), BF16),
             pltpu.VMEM((cohorts, 1, rows), F32),
             pltpu.VMEM((1, rows), F32),
+            pltpu.VMEM((1, rows), F32),
             pltpu.VMEM((traits, width), F32),
             dma((CHUNKS,)),
             dma((CHUNKS,)),

time: 131 us -> 131 us (level); the launches traced: 130 us -> 132 us
  Pallas kernels: 94.7 us -> 96.7 us
    pallas_call x2, Pallas kernels: 30.2 us -> 32.5 us  [by_gene(): pl.pallas_call(kernel, grid_spec=pltpu.PrefetchScalarGridSpec(num_scalar_...]
  transfers between devices with their start and end apart: 2 -> 2, of which waited for: 0 -> 0; matrix products, arithmetic and copies ran while one was open for 20% -> 19% of each run, Pallas kernels for 27% -> 27%
where the time goes in v4:
time: 131 us; the launch traced here: 132 us
  Pallas kernels  96.7 us (74%)
  local copies, waits for them, and re-layouts  17.7 us (14%)
  other arithmetic  10.2 us (8%)
  starting transfers between devices  7.08 us (5%)
    pallas_call x1, Pallas kernels, combine(): pl.pallas_call(functools.partial(combine_kernel, z_count, traits), out_sh...  47 us
    pallas_call x2, Pallas kernels, by_gene(): pl.pallas_call(kernel, grid_spec=pltpu.PrefetchScalarGridSpec(num_scalar_...  32.5 us
    pallas_call x1, Pallas kernels, pack_rows(): pl.pallas_call(pack_kernel, grid_spec=pltpu.PrefetchScalarGridSpec(num_sc...  17.2 us
    unnamed x9, local copies, waits for them, and re-layouts  14.7 us
    all_to_all x1, starting transfers between devices, fast_device(): lax.all_to_all(outgoing, 'stripe', split_axis=0, concat_axis=0, tiled=True)  5.15 us
  transfers between devices with their start and end apart: 2, of which 0 were waited for; matrix products, arithmetic and copies ran while one was open for 19% of the time, Pallas kernels for 27%

profile of v4, /device:TPU:1, one launch (start us, length us, event | category | flops | bytes accessed | tf_op | source)
XLA Modules:
  0.0 131.8 jit_solution(9329593469448277597)
XLA Ops:
  0.0 1.1 constant_dynamic-slice_fusion
  1.1 1.9 %collective-permute-start = (bf16[64,4608]{1,0:T(8,128)(2,1)S(1)}, bf16[64,4608]{1,0:T(8,128)(2,1)}, u32[]{:S(2)}, u32[]{:S(2)}) collective-permute-start(bf16[64,4608]{1,0:T(8,128)(2,1)S(1)} %constant_dynamic-slice_fusion), channel_id=1, source_target_pairs={{1,0},{2,1},{3,2},{5,4},{6,5},{7,6},{9,8},{10,9},{11,10},{13,12},{... | collective-permute-start | bytes 1769480 | tf_op jit(solution)/shard_map/ppermute | solution.py:16
  3.1 0.9 fusion.5
  4.0 0.9 fusion.7
  4.8 0.9 fusion.8
  5.8 1.2 reduce-window.6
  6.9 0.2 slice_reduce_fusion
  7.2 0.2 reduce-window.9
  7.4 0.1 select_reduce_fusion
  7.5 0.0 copy-start.1
  7.5 0.1 slice.11
  7.6 0.2 convert_reduce_fusion.1
  7.9 0.1 copy.14
  8.0 0.7 reshape.68.low_ref
  8.6 0.1 copy.15
  8.7 0.7 add.33.high_ref
  9.4 2.8 %copy.16 = bf16[1,4608,256]{1,2,0:T(8,128)(2,1)S(1)} copy(bf16[1,4608,256]{2,1,0:T(8,128)(2,1)} %param.8) | data formatting | bytes 4718592 | tf_op args[0]
  12.3 0.1 convert_reduce_fusion
  12.4 0.2 fusion
  12.5 0.1 pad.3.clone
  12.6 0.6 fusion.4.slot_ref
  13.2 2.0 %maximum_maximum_fusion.left_ref = bf16[272,4608]{1,0:T(8,128)(2,1)} fusion(bf16[1,4608]{1,0:T(2,128)(2,1)S(1)} %convert_element_type.37, bf16[1,4608]{1,0:T(2,128)(2,1)S(1)} %get-tuple-element.17, bf16[256,4608]{1,0:T(8,128)(2,1)S(1)} %fusion, bf16[272]{0:T(512)(128)(2,1)S(1)} %pad.3.clone), kind=kLoop, calls=%fused_computation | loop fusion | flops 10027008 | bytes 4885024 | tf_op jit(solution)/shard_map/concatenate | solution.py:608
  15.3 17.2 %shard_map.83 = bf16[4,272,1152]{2,1,0:T(8,128)(2,1)} custom-call(s32[12]{0:T(128)} %reshape.68.low_ref, s32[12]{0:T(128)} %add.33.high_ref, bf16[272,4608]{1,0:T(8,128)(2,1)} %maximum_maximum_fusion.left_ref, f32[36,128]{1,0:T(8,128)} %fusion.4.slot_ref), custom_call_target="tpu_custom_call" | custom-call | flops 5775556608 | bytes 5013504 | tf_op jit(solution)/shard_map/pallas_call | solution.py:197
  32.5 5.2 %all-to-all-start = ((bf16[4,272,1152]{2,1,0:T(8,128)(2,1)}), bf16[4,272,1152]{2,1,0:T(8,128)(2,1)S(1)}, u32[]{:S(2)}, u32[]{:S(2)}) async-start(bf16[4,272,1152]{2,1,0:T(8,128)(2,1)} %shard_map.83), calls=%async_computation | async-start | bytes 5013504 | tf_op jit(solution)/shard_map/all_to_all | solution.py:624
  37.6 10.3 %copy.13.weight_ref = bf16[16,49,4608]{2,1,0:T(8,128)(2,1)} copy(bf16[16,49,4608]{2,0,1:T(8,128)(2,1)} %param.13) | data formatting | bytes 14450688 | tf_op args[5]
  48.0 0.5 broadcast_subtract_fusion.begin_ref
  48.5 2.3 %maximum_maximum_fusion.1.side_ref = bf16[64,10368]{1,0:T(8,128)(2,1)} fusion(bf16[64,4608]{1,0:T(8,128)(2,1)} %collective-permute-done, bf16[64,4608]{1,0:T(8,128)(2,1)S(1)} %constant_dynamic-slice_fusion, bf16[10368]{0:T(1024)(128)(2,1)S(1)} %pad.6.clone), kind=kLoop, calls=%fused_computation.3 | loop fusion | flops 3981312 | bytes 2527488 | tf_op jit(solution)/shard_map/concatenate | solution.py:567
  50.9 18.9 %shard_map.82 = (f32[16,1,49]{2,1,0:T(1,128)}, bf16[16,49,5760]{2,1,0:T(8,128)(2,1)}) custom-call(s32[16]{0:T(128)} %broadcast_subtract_fusion.begin_ref, s32[16]{0:T(128)} %size_ref.3, bf16[16,49,4608]{2,1,0:T(8,128)(2,1)} %copy.13.weight_ref, bf16[64,10368]{1,0:T(8,128)(2,1)} %maximum_maximum_fusion.1.side_ref), custom_call_target="tpu_custom_call" | custom-call | flops 3699376128 | bytes 14450688 | tf_op jit(solution)/shard_map/pallas_call | solution.py:543
  69.8 0.0 all-to-all-done.got_ref
  69.8 1.5 %copy-done = bf16[4,272,1152]{2,1,0:T(8,128)(2,1)} copy-done((bf16[4,272,1152]{2,1,0:T(8,128)(2,1)}, bf16[4,272,1152]{2,1,0:T(8,128)(2,1)S(1)}, u32[]{:S(2)}) %copy-start) | copy-done | bytes 2506776
  71.2 47.0 %shard_map.84 = (bf16[32,10368]{1,0:T(8,128)(2,1)}, f32[16,1,49]{2,1,0:T(1,128)}) custom-call(bf16[4,272,1152]{2,1,0:T(8,128)(2,1)} %copy-done, f32[1,4608]{1,0:T(1,128)} %precision_ref.1, f32[16,1,49]{2,1,0:T(1,128)} %get-tuple-element.10.square_ref), custom_call_target="tpu_custom_call" | custom-call | tf_op jit(solution)/shard_map/pallas_call | solution.py:427
  118.2 13.6 %shard_map.85 = f32[16,32,49]{2,1,0:T(8,128)} custom-call(s32[16]{0:T(128)} %broadcast_subtract_fusion.begin_ref, s32[16]{0:T(128)} %size_ref.3, bf16[16,49,5760]{2,1,0:T(8,128)(2,1)} %get-tuple-element.9.aligned_ref, bf16[32,10368]{1,0:T(8,128)(2,1)} %get-tuple-element.11.side_ref, f32[16,1,49]{2,1,0:T(1,128)} %get-tuple-element.12.square_ref), custom_call_target="tpu_custom_call" | custom-call | flops 2312110080 | bytes 18063360 | tf_op jit(solution)/shard_map/pallas_call | solution.py:543
  (13 shorter events, 0.1 us)
Async XLA Ops:
  1.1 47.4 %collective-permute-start = (bf16[64,4608]{1,0:T(8,128)(2,1)S(1)}, bf16[64,4608]{1,0:T(8,128)(2,1)}, u32[]{:S(2)}, u32[]{:S(2)}) collective-permute-start(bf16[64,4608]{1,0:T(8,128)(2,1)S(1)} %constant_dynamic-slice_fusion), channel_id=1, source_target_pairs={{1,0},{2,1},{3,2},{5,4},{6,5},{7,6},{9,8},{10,9},{11,10},{13,12},{... | collective-permute-start | bytes 1769480 | tf_op jit(solution)/shard_map/ppermute | solution.py:16
  7.5 4.8 %copy-start.1 = (s32[1,4608]{1,0:T(1,128)S(1)}, s32[1,4608]{1,0:T(1,128)}, u32[]{:S(2)}) copy-start(s32[1,4608]{1,0:T(1,128)} %param.10) | copy-start | bytes 55300
  32.5 37.3 %all-to-all-start = ((bf16[4,272,1152]{2,1,0:T(8,128)(2,1)}), bf16[4,272,1152]{2,1,0:T(8,128)(2,1)S(1)}, u32[]{:S(2)}, u32[]{:S(2)}) async-start(bf16[4,272,1152]{2,1,0:T(8,128)(2,1)} %shard_map.83), calls=%async_computation | async-start | bytes 5013504 | tf_op jit(solution)/shard_map/all_to_all | solution.py:624
  37.6 10.3 %copy-start.2 = (s32[16]{0:T(128)S(1)}, s32[16]{0:T(128)}, u32[]{:S(2)}) copy-start(s32[16]{0:T(128)} %param.14) | copy-start | bytes 196
  69.8 1.5 %copy-start = (bf16[4,272,1152]{2,1,0:T(8,128)(2,1)}, bf16[4,272,1152]{2,1,0:T(8,128)(2,1)S(1)}, u32[]{:S(2)}) copy-start(bf16[4,272,1152]{2,1,0:T(8,128)(2,1)S(1)} %all-to-all-done.got_ref) | copy-start | bytes 7520260
